TPU v7x, 128 devices: a whole 4x4x4 slice. The times are simulated.
128 devices in a mesh: row: 16 (over y_lo, x, core), col: 8 (over y_hi, z).
Axes of the slice: x: 4, y: 4 (y_hi: 2, y_lo: 2; y = y_hi * 2 + y_lo), z: 4, core: 2. Of those that a mesh axis runs over, the one named last changes fastest.
Arguments:
- cholesky_vectors: float32 [256, 512, 512], P(('row', 'col')), as said below
- factor: float32 [512, 2048], P(('row', 'col')), may hold values from -0.25 to 0.25
- core_weights: float32 [256, 2048], P(('row', 'col')), may hold values from -0.375 to 0.375
Outputs:
- core_gradient: float32 [256, 2048], P(('row', 'col'))
- factor_gradient: float32 [512, 2048], P('row', 'col')
Inputs may be any that keep to these rules, and one draw needn't show every extreme that they name: Each cholesky_vectors[P] is symmetric.
All inputs are finite; a program needn't handle non-finite values.
Results may differ from a plain program's by a relative error of at most 0.0001.
Values sent between devices are 32-bit elements; how exact they have to be, the bound alone decides.
A program may use at most 384 MiB of HBM per device.

v0:
```python
import jax
import jax.numpy as jnp
from jax import lax
from jax.sharding import PartitionSpec as P


def on_device(cholesky_vectors, factor, core_weights):
    high = lax.Precision.HIGHEST
    vectors = cholesky_vectors.shape[0]
    orbitals = cholesky_vectors.shape[1]
    rank = factor.shape[1]
    piece = lax.all_gather(factor, ("row", "col"), axis=0, tiled=True)
    adjoint = jnp.einsum(
        "pba,bc->pac", cholesky_vectors, piece, precision=high, preferred_element_type=jnp.float32
    )
    assembled = piece
    projection = jnp.sum(assembled[None] * adjoint, axis=1)
    adjoint_sum = jnp.sum(adjoint * core_weights[:, None, :], axis=0)
    row_count = lax.axis_size("row")
    col_count = lax.axis_size("col")
    row_width = rank // row_count
    col_width = rank // col_count
    orb_width = orbitals // row_count
    row_index = lax.axis_index("row")
    col_index = lax.axis_index("col")

    def tile(tile_index):
        row_block = tile_index // col_count
        col_block = tile_index % col_count
        left = lax.dynamic_slice_in_dim(core_weights, row_block * row_width, row_width, 1)
        right = lax.dynamic_slice_in_dim(core_weights, col_block * col_width, col_width, 1)
        return jnp.dot(left.T, right, precision=high, preferred_element_type=jnp.float32)

    weight_tile = lax.psum_scatter(
        jax.vmap(tile)(jnp.arange(1 * lax.axis_size(("row", "col")), dtype=jnp.int32)),
        ("row", "col"),
        scatter_dimension=0,
        tiled=True,
    )[0]
    row_cols = lax.dynamic_slice_in_dim(assembled, row_index * row_width, row_width, 1)
    col_cols = lax.dynamic_slice_in_dim(assembled, col_index * col_width, col_width, 1)
    gram_tile = jnp.dot(row_cols.T, col_cols, precision=high, preferred_element_type=jnp.float32)
    mixed_tile = gram_tile * weight_tile
    square_tile = gram_tile * gram_tile
    empty = jnp.zeros((vectors, rank), jnp.float32)
    piece = lax.all_gather(square_tile[None], ("row", "col"), axis=0, tiled=True)

    def one_tile(turn, accum):
        row_block = turn // col_count
        col_block = turn % col_count
        left = lax.dynamic_slice_in_dim(core_weights, row_block * row_width, row_width, 1)
        product = jnp.dot(left, piece[turn], precision=high, preferred_element_type=jnp.float32)
        current = lax.dynamic_slice_in_dim(accum, col_block * col_width, col_width, 1)
        return lax.dynamic_update_slice_in_dim(accum, current + product, col_block * col_width, 1)

    weighted = lax.fori_loop(0, piece.shape[0], one_tile, empty)
    core_gradient = weighted - projection
    partial_rows = jnp.dot(row_cols, mixed_tile, precision=high, preferred_element_type=jnp.float32)

    def adjoint_block(tile_index):
        row_block = tile_index // col_count
        col_block = tile_index % col_count
        rows = lax.dynamic_slice_in_dim(adjoint_sum, row_block * orb_width, orb_width, 0)
        return (
            lax.dynamic_slice_in_dim(rows, col_block * col_width, col_width, 1),
            row_block,
            col_block,
        )

    summed_rows = lax.psum_scatter(partial_rows, "row", scatter_dimension=0, tiled=True)
    blocks = jax.vmap(adjoint_block)(jnp.arange(1 * lax.axis_size(("row", "col")), dtype=jnp.int32))
    summed_adjoint = lax.psum_scatter(blocks[0], ("row", "col"), scatter_dimension=0, tiled=True)[0]
    factor_gradient = 4.0 * (summed_rows - summed_adjoint)
    return (core_gradient, factor_gradient)


def solution(mesh):
    placed = (P(("row", "col"), None, None), P(("row", "col"), None), P(("row", "col"), None))
    return jax.shard_map(
        on_device,
        mesh=mesh,
        in_specs=placed,
        out_specs=(P(("row", "col"), None), P("row", "col")),
        check_vma=False,
    )
```

profile of v0, /device:TPU:0, one launch (start us, length us, event | category | flops | bytes accessed | tf_op | source)
XLA Modules:
  0.0 2400.4 jit_solution(16267583942759927890)
XLA Ops:
  8.0 268.2 %while.20 = (s32[]{:T(128)}, f32[2,2048]{1,0:T(2,128)}, s32[128,2]{0,1:T(2,128)S(1)}, f32[128,2,256]{2,1,0:T(2,128)S(1)}, s32[]{:T(128)}) while((s32[]{:T(128)}, f32[2,2048]{1,0:T(2,128)}, s32[128,2]{0,1:T(2,128)S(1)}, f32[128,2,256]{2,1,0:T(2,128)S(1)}, s32[]{:T(128)}) %tuple.82), condition=%wide.while_cond.1, body=%wide.while_body.1.sunk | while | flops 2 | bytes 4201 | solution.py:31
  276.2 255.8 %while.19 = (s32[]{:T(128)}, f32[2,2048]{1,0:T(2,128)}, s32[128,2]{0,1:T(2,128)S(1)}, f32[128,2,128]{2,1,0:T(2,128)S(1)}, s32[]{:T(128)}) while((s32[]{:T(128)}, f32[2,2048]{1,0:T(2,128)}, s32[128,2]{0,1:T(2,128)S(1)}, f32[128,2,128]{2,1,0:T(2,128)S(1)}, s32[]{:T(128)}) %tuple.98), condition=%wide.while_cond, body=%wide.while_body.sunk | while | flops 2 | bytes 2153 | solution.py:30
  532.1 16.2 fusion.15
  548.6 5.3 reshape.158
  553.9 5.3 reshape.159
  559.3 19.0 multiply_reduce_fusion
  578.3 376.5 %while.21 = (s32[]{:T(128)}, f32[512,2048]{1,0:T(8,128)}, s32[128,2]{0,1:T(2,128)S(1)}, f32[128,32,2048]{2,1,0:T(8,128)}, s32[]{:T(128)}) while((s32[]{:T(128)}, f32[512,2048]{1,0:T(8,128)}, s32[128,2]{0,1:T(2,128)S(1)}, f32[128,32,2048]{2,1,0:T(8,128)}, s32[]{:T(128)}) %tuple.85), condition=%wide.while_cond.2, body=%wide.while_body.2.sunk | while | flops 2 | bytes 524901 | solution.py:63
  590.6 2.4 bitcast_dynamic-update-slice_fusion.8
  608.2 2.4 bitcast_dynamic-update-slice_fusion.8
  611.2 2.4 bitcast_dynamic-update-slice_fusion.8
  614.1 2.4 bitcast_dynamic-update-slice_fusion.8
  628.8 2.4 bitcast_dynamic-update-slice_fusion.8
  655.3 2.4 bitcast_dynamic-update-slice_fusion.8
  658.3 2.4 bitcast_dynamic-update-slice_fusion.8
  670.0 2.4 bitcast_dynamic-update-slice_fusion.8
  675.9 2.4 bitcast_dynamic-update-slice_fusion.8
  678.9 2.4 bitcast_dynamic-update-slice_fusion.8
  681.9 2.4 bitcast_dynamic-update-slice_fusion.8
  696.6 2.4 bitcast_dynamic-update-slice_fusion.8
  699.5 2.4 bitcast_dynamic-update-slice_fusion.8
  723.0 2.4 bitcast_dynamic-update-slice_fusion.8
  758.3 2.4 bitcast_dynamic-update-slice_fusion.8
  778.9 2.4 bitcast_dynamic-update-slice_fusion.8
  796.6 2.4 bitcast_dynamic-update-slice_fusion.8
  799.5 2.4 bitcast_dynamic-update-slice_fusion.8
  817.2 2.4 bitcast_dynamic-update-slice_fusion.8
  820.1 2.4 bitcast_dynamic-update-slice_fusion.8
  843.6 2.4 bitcast_dynamic-update-slice_fusion.8
  846.6 2.4 bitcast_dynamic-update-slice_fusion.8
  858.4 2.4 bitcast_dynamic-update-slice_fusion.8
  861.3 2.4 bitcast_dynamic-update-slice_fusion.8
  864.3 2.4 bitcast_dynamic-update-slice_fusion.8
  867.3 2.4 bitcast_dynamic-update-slice_fusion.8
  870.2 2.4 bitcast_dynamic-update-slice_fusion.8
  884.9 2.4 bitcast_dynamic-update-slice_fusion.8
  887.9 2.4 bitcast_dynamic-update-slice_fusion.8
  905.5 2.4 bitcast_dynamic-update-slice_fusion.8
  908.5 2.4 bitcast_dynamic-update-slice_fusion.8
  911.4 2.4 bitcast_dynamic-update-slice_fusion.8
  954.8 98.5 %copy.9 = f32[128,32,2048]{1,0,2:T(8,128)} copy(f32[128,32,2048]{2,1,0:T(8,128)} %get-tuple-element.139) | data formatting | bytes 67108864 | tf_op jit(solution)/shard_map/vmap()/gather | solution.py:63
  1053.3 30.0 %gather_fusion = f32[128,32,256]{1,0,2:T(8,128)} fusion(f32[128,32,2048]{1,0,2:T(8,128)} %copy.9, s32[128]{0:T(128)S(1)} %or_bitcast_fusion), kind=kCustom, calls=%fused_computation | custom fusion | bytes 8390144 | tf_op jit(solution)/shard_map/vmap()/gather | solution.py:65
  1083.3 13.4 copy.10
  1096.8 2.4 fusion.14
  1099.2 128.7 %reduce-scatter.4.cloned.1.call-done = f32[1,128,256]{2,1,0:T(8,128)} async-done(((f32[128,128,256]{2,1,0:T(8,128)}), f32[1,128,256]{2,1,0:T(8,128)}) %reduce-scatter.4.cloned.1.call-update) | async-done | bytes 131088 | tf_op jit(solution)/shard_map/reduce_scatter | solution.py:34
  1230.9 644.0 %reduce-scatter.8.cloned.1.call-done = f32[1,32,256]{2,1,0:T(8,128)} async-done(((f32[128,32,256]{2,1,0:T(8,128)}), f32[1,32,256]{2,1,0:T(8,128)}) %reduce-scatter.8.cloned.1.call-update) | async-done | bytes 32784 | tf_op jit(solution)/shard_map/reduce_scatter | solution.py:72
  1874.8 57.8 %reduce-scatter.6.cloned.1.call-done = f32[32,256]{1,0:T(8,128)} async-done(((f32[512,256]{1,0:T(8,128)}), f32[32,256]{1,0:T(8,128)}) %reduce-scatter.6.cloned.1.call-update) | async-done | bytes 32784 | tf_op jit(solution)/shard_map/reduce_scatter | solution.py:70
  1934.0 320.8 %all-gather.5.cloned.1.call-done = f32[16384,256]{1,0:T(8,128)} async-done(((f32[128,256]{1,0:T(8,128)}), f32[16384,256]{1,0:T(8,128)}) %all-gather.5.cloned.1.call-update) | async-done | bytes 16777232 | tf_op jit(solution)/shard_map/all_gather | solution.py:46
  2254.9 138.4 %while.18 = (s32[]{:T(128)}, f32[2,2048]{1,0:T(2,128)S(1)}, f32[2,2048]{1,0:T(2,128)S(1)}, f32[128,128,256]{2,1,0:T(8,128)}, s32[]{:T(128)}, /*index=5*/s32[]{:T...) while((s32[]{:T(128)}, f32[2,2048]{1,0:T(2,128)S(1)}, ...), condition=%wide.region_1.0_spmd, body=%wide.region_0.0_spmd.sunk | while | flops 786966 | bytes 136544 | solution.py:56
  (1278 shorter events, 968.5 us)
Async XLA Ops:
  7.2 552.1 %copy-start = (f32[2,512,512]{2,1,0:T(8,128)S(1)}, f32[2,512,512]{2,1,0:T(8,128)}, u32[]{:S(2)}) copy-start(f32[2,512,512]{2,1,0:T(8,128)} %param.5) | copy-start | bytes 6291460
  7.2 541.4 %all-gather.7.cloned.1.call-start = ((), (), s32[]{:S(2)}) async-start(), calls=%async_computation.7 | async-start | bytes 4227072 | tf_op jit(solution)/shard_map/all_gather | solution.py:12
  7.9 1220.0 %reduce-scatter.4.cloned.1.call-start = ((), (), s32[]{:S(2)}) async-start(), calls=%async_computation.3 | async-start | bytes 16908288 | tf_op jit(solution)/shard_map/reduce_scatter | solution.py:34
  548.3 1326.6 %reduce-scatter.8.cloned.1.call-start = ((), (), s32[]{:S(2)}) async-start(), calls=%async_computation.5 | async-start | bytes 4227072 | tf_op jit(solution)/shard_map/reduce_scatter | solution.py:72
  553.9 5.3 copy-start.2
  1083.3 1310.6 %copy-start.1 = (f32[2,512,512]{2,1,0:T(8,128)S(1)}, f32[2,512,512]{2,1,0:T(8,128)}, u32[]{:S(2)}) copy-start(f32[2,512,512]{2,1,0:T(8,128)} %param.5) | copy-start | bytes 6291460
  1096.7 835.9 %reduce-scatter.6.cloned.1.call-start = ((), (), s32[]{:S(2)}) async-start(), calls=%async_computation.4 | async-start | bytes 557056 | tf_op jit(solution)/shard_map/reduce_scatter | solution.py:70
  1230.3 1024.6 %all-gather.5.cloned.1.call-start = ((), (), s32[]{:S(2)}) async-start(), calls=%async_computation.6 | async-start | bytes 16908288 | tf_op jit(solution)/shard_map/all_gather | solution.py:46
Sparse Core Ops, SparseCore 0:
  9.7 305.2 all-gather.6
  548.4 679.4 reduce-scatter.3
  1230.3 644.5 reduce-scatter.7
  1877.0 55.5 reduce-scatter.5
  1934.2 320.6 all-gather.4
where the time goes:
time: 2420 us; the launch traced here: 2400 us
  waiting for transfers between devices  1150 us (48%)
  local copies, waits for them, and re-layouts  1050 us (43%)
  matrix products  178 us (7%)
    gather x1152, local copies, waits for them, and re-layouts  900 us
    reduce_scatter x1, waiting for transfers between devices, on_device(): lax.psum_scatter(blocks[0], ('row', 'col'), scatter_dimension=0, tiled=True)  644 us
    all_gather x1, waiting for transfers between devices, on_device(): lax.all_gather(square_tile[None], ('row', 'col'), axis=0, tiled=True)  321 us
    dot_general x128, matrix products, one_tile(): jnp.dot(left, piece[turn], precision=high, preferred_element_type=jnp.flo...  138 us
    reduce_scatter x1, waiting for transfers between devices, on_device(): lax.psum_scatter(jax.vmap(tile)(jnp.arange(1 * lax.axis_size(('row', 'col...  129 us
    gather x1, local copies, waits for them, and re-layouts, adjoint_block(): lax.dynamic_slice_in_dim(adjoint_sum, row_block * orb_width, orb_width, 0)  98.5 us
    reduce_scatter x1, waiting for transfers between devices, on_device(): lax.psum_scatter(partial_rows, 'row', scatter_dimension=0, tiled=True)  57.8 us
  transfers between devices with their start and end apart: 5, of which 4 were waited for; matrix products, arithmetic and copies ran while one was open for 46% of the time, Pallas kernels for 0%

commit v1 on v0

v1 whole, which is shorter than its diff:
```python
import jax
import jax.numpy as jnp
from jax import lax
from jax.sharding import PartitionSpec as P

AXES = ("row", "col")


def on_device(cholesky_vectors, factor, core_weights):
    high = lax.Precision.HIGHEST
    rank = factor.shape[1]
    rows, cols = lax.axis_size("row"), lax.axis_size("col")
    r, c = lax.axis_index("row"), lax.axis_index("col")
    x = lax.all_gather(factor, AXES, axis=0, tiled=True)
    z = lax.all_gather(core_weights, AXES, axis=0, tiled=True)
    orbitals, width = x.shape[0], rank // cols

    def dot(a, b, dims):
        return lax.dot_general(a, b, (dims, ((), ())), precision=high, preferred_element_type=jnp.float32)

    adjoint = jnp.einsum("pab,bc->pac", cholesky_vectors, x, precision=high, preferred_element_type=jnp.float32)
    projection = jnp.sum(x[None] * adjoint, axis=1)
    part = jnp.sum(adjoint * core_weights[:, None, :], axis=0)
    part = part.reshape(rows, orbitals // rows, cols, width).transpose(0, 2, 1, 3)
    part = part.reshape(rows * cols, orbitals // rows, width)
    summed = lax.psum_scatter(part, AXES, scatter_dimension=0, tiled=True)[0]

    x_c = lax.dynamic_slice_in_dim(x, c * width, width, 1)
    z_c = lax.dynamic_slice_in_dim(z, c * width, width, 1)
    gram = dot(x_c, x, ((0,), (0,)))
    core_gram = dot(z_c, z, ((0,), (0,)))
    x_r = lax.dynamic_slice_in_dim(x, r * (orbitals // rows), orbitals // rows, 0)
    z_r = lax.dynamic_slice_in_dim(z, r * (z.shape[0] // rows), z.shape[0] // rows, 0)
    first = dot(x_r, gram * core_gram, ((1,), (1,)))
    weighted = dot(z_r, gram * gram, ((1,), (1,)))
    own = lax.all_to_all(weighted, "col", split_axis=0, concat_axis=1, tiled=True)
    return own - projection, 4.0 * (first - summed)


def solution(mesh):
    placed = (P(AXES, None, None), P(AXES, None), P(AXES, None))
    return jax.shard_map(
        on_device, mesh=mesh, in_specs=placed, out_specs=(P(AXES, None), P("row", "col")), check_vma=False
    )
```

time: 2420 us -> 1290 us (0.53)
  local copies, waits for them, and re-layouts: 1050 us -> 21.9 us
  matrix products: 178 us -> 34.8 us
  waiting for transfers between devices: 1150 us -> 1210 us
    gather x1155 -> x0, local copies, waits for them, and re-layouts: 1040 us -> none
    all_gather x2, waiting for transfers between devices: 321 us -> 579 us  [the longest x1 307 us: on_device(): x = lax.all_gather(factor, AXES, axis=0, tiled=True)]
    reduce_scatter x3 -> x1, waiting for transfers between devices: 830 us -> 627 us  [on_device(): summed = lax.psum_scatter(part, AXES, scatter_dimension=0, tiled=True)[0]]
    dot_general x132 -> x5, matrix products: 178 us -> 34.8 us  [the longest x4 17.8 us: dot(): lax.dot_general(a, b, (dims, ((), ())), precision=high, preferred_element...]
  transfers between devices with their start and end apart: 5 -> 4, of which waited for: 4 -> 4; matrix products, arithmetic and copies ran while one was open for 46% -> 4% of each run, Pallas kernels for 0% -> 0%
where the time goes in v1:
time: 1290 us
  waiting for transfers between devices  1210 us (94%)
  matrix products  34.8 us (3%)
  local copies, waits for them, and re-layouts  21.9 us (2%)
  between operations  13.8 us (1%)
    reduce_scatter x1, waiting for transfers between devices, on_device(): summed = lax.psum_scatter(part, AXES, scatter_dimension=0, tiled=True)[0]  627 us
    all_gather x1, waiting for transfers between devices, on_device(): x = lax.all_gather(factor, AXES, axis=0, tiled=True)  307 us
    all_gather x1, waiting for transfers between devices, on_device(): z = lax.all_gather(core_weights, AXES, axis=0, tiled=True)  272 us
  transfers between devices with their start and end apart: 4, of which 4 were waited for; matrix products, arithmetic and copies ran while one was open for 4% of the time, Pallas kernels for 0%

profile of v1, /device:TPU:0, one launch (start us, length us, event | category | flops | bytes accessed | tf_op | source)
XLA Modules:
  0.0 1287.9 jit_solution(15794297128244354943)
XLA Ops:
  7.2 0.0 copy-start
  7.2 0.0 all-gather.7.cloned.1.call-start
  7.2 0.7 all-gather.7.cloned.1.call-update
  7.9 0.0 all-gather.5.cloned.1.call-start
  8.0 0.7 all-gather.5.cloned.1.call-update
  8.7 0.0 reduce-scatter.2.cloned.1.call-start
  8.7 307.2 %all-gather.7.cloned.1.call-done = f32[128,4,2048]{2,1,0:T(4,128)} async-done(((f32[1,4,2048]{2,1,0:T(4,128)}), f32[128,4,2048]{2,1,0:T(4,128)}) %all-gather.7.cloned.1.call-update) | async-done | bytes 4194320 | tf_op jit(solution)/shard_map/all_gather | solution.py:14
  315.9 5.3 reshape.20
  321.2 0.0 copy-start.2
  321.2 5.3 reshape.21
  326.5 0.0 copy-done
  326.5 0.0 copy-done.2
  326.5 17.0 %multiply_reduce_fusion = (f32[512,2048]{1,0:T(8,128)S(1)}, f32[2,2048]{1,0:T(2,128)S(1)}) fusion(f32[2,2048]{1,0:T(2,128)S(1)} %copy-done.2, f32[512,2048]{1,0:T(8,128)} %reshape.20, f32[2,512,512]{2,1,0:T(8,128)S(1)} %copy-done, f32[512,2048,1]{1,0,2:T(8,128)} %reshape.21), kind=kOutput, calls=%fused_computation | convolution fusion | flops 12892237824 | bytes 14712832 | tf_op jit(solution)/shard_map/pab,bc->pac/dot_general | solution.py:21
  343.6 2.0 copy.10
  345.5 0.4 bitcast_bitcast_fusion
  345.9 3.3 copy.9
  349.2 0.0 reduce-scatter.2.cloned.1.call-update
  349.2 272.3 %all-gather.5.cloned.1.call-done = f32[128,2,2048]{2,1,0:T(2,128)} async-done(((f32[1,2,2048]{2,1,0:T(2,128)}), f32[128,2,2048]{2,1,0:T(2,128)}) %all-gather.5.cloned.1.call-update) | async-done | bytes 2097168 | tf_op jit(solution)/shard_map/all_gather | solution.py:15
  621.5 3.7 reshape.18
  625.2 5.5 fusion.3
  630.7 0.0 copy-start.1
  630.7 1.3 copy-done.1
  632.0 2.6 fusion
  634.6 0.6 all_to_all.14
  635.3 6.7 all-to-all-start
  642.0 5.6 convolution_multiply_fusion
  647.6 2.2 all-to-all-done
  649.7 0.6 sub.6
  650.3 626.9 %reduce-scatter.2.cloned.1.call-done = f32[1,32,256]{2,1,0:T(8,128)} async-done(((f32[128,32,256]{2,1,0:T(8,128)}), f32[1,32,256]{2,1,0:T(8,128)}) %reduce-scatter.2.cloned.1.call-update) | async-done | bytes 32784 | tf_op jit(solution)/shard_map/reduce_scatter | solution.py:26
  1277.3 4.1 fusion.2
Async XLA Ops:
  7.2 319.4 %copy-start = (f32[2,512,512]{2,1,0:T(8,128)S(1)}, f32[2,512,512]{2,1,0:T(8,128)}, u32[]{:S(2)}) copy-start(f32[2,512,512]{2,1,0:T(8,128)} %param.3) | copy-start | bytes 6291460
  7.2 308.7 %all-gather.7.cloned.1.call-start = ((), (), s32[]{:S(2)}) async-start(), calls=%async_computation.4 | async-start | bytes 4227072 | tf_op jit(solution)/shard_map/all_gather | solution.py:14
  7.9 613.6 %all-gather.5.cloned.1.call-start = ((), (), s32[]{:S(2)}) async-start(), calls=%async_computation.3 | async-start | bytes 2113536 | tf_op jit(solution)/shard_map/all_gather | solution.py:15
  8.7 1268.6 %reduce-scatter.2.cloned.1.call-start = ((), (), s32[]{:S(2)}) async-start(), calls=%async_computation.2 | async-start | bytes 4227072 | tf_op jit(solution)/shard_map/reduce_scatter | solution.py:26
  321.2 5.3 copy-start.2
  630.7 1.3 copy-start.1
  635.3 14.4 %all-to-all-start = ((f32[8,2,256]{2,1,0:T(2,128)}), f32[8,2,256]{2,1,0:T(2,128)S(1)}, u32[]{:S(2)}, u32[]{:S(2)}) async-start(f32[8,2,256]{2,1,0:T(2,128)} %all_to_all.14), calls=%async_computation | async-start | bytes 32768 | tf_op jit(solution)/shard_map/all_to_all | solution.py:36
Sparse Core Ops, SparseCore 0:
  9.7 306.1 all-gather.6
  317.6 303.8 all-gather.4
  623.9 653.3 reduce-scatter.1

commit v2 on v1

v2 whole, which is shorter than its diff:
```python
import functools

import jax
import jax.numpy as jnp
from jax import lax
from jax.experimental import pallas as pl
from jax.experimental.pallas import tpu as pltpu
from jax.sharding import PartitionSpec as P

AXES = ("row", "col")
F32, BF16 = jnp.float32, jnp.bfloat16
MESH = pl.DeviceIdType.MESH

ORDERS = ("xyz", "yzx", "zxy")
X_PARTS = ((pl.ds(0, 8), pl.ds(0, 384)), (pl.ds(8, 8), pl.ds(0, 384)), (pl.ds(0, 16), pl.ds(384, 128)))
Z_PARTS = ((pl.ds(0, 8), pl.ds(0, 128)), (pl.ds(0, 8), pl.ds(128, 128)), (pl.ds(0, 8), pl.ds(256, 256)))
S_PARTS = ((pl.ds(0, 24), pl.ds(0, 128)), (pl.ds(0, 24), pl.ds(128, 128)), (pl.ds(24, 8), pl.ds(0, 256)))


def split(value):
    hi = value.astype(BF16)
    return hi, (value - hi.astype(F32)).astype(BF16)


def dot(a, b):
    return lax.dot_general(a, b, (((1,), (0,)), ((), ())), preferred_element_type=F32)


def dot_nt(a, b):
    return lax.dot_general(a, b, (((1,), (1,)), ((), ())), preferred_element_type=F32)


def kernel(
    x_ref, z_ref, l_hbm, core_out, factor_out,
    lbuf, lcat, xs, zs, xb, zb, xcat, zcat, xct, zct, proj,
    psend, precv, s_buf, f_minus, f_plus, r_minus, r_plus, r_two, r_three,
    first, weighted, ks, kb, lsem, send, recv,
):
    r, c = lax.axis_index("row"), lax.axis_index("col")
    k = lax.rem(r, 2)
    me = {
        "x": lax.rem(r // 2, 4),
        "y": (c // 4) * 2 + r // 8,
        "z": lax.rem(c, 4),
    }

    def device(x, y, z, core):
        return ((lax.rem(y, 2) * 4 + x) * 2 + core, (y // 2) * 4 + z)

    def at(axis, d):
        return lax.rem(me[axis] + d, 4)

    def peer(axis, d):
        where = dict(me)
        where[axis] = at(axis, d)
        return device(where["x"], where["y"], where["z"], k)

    partner = device(me["x"], me["y"], me["z"], 1 - k)
    ids, started = {}, []

    def sem_of(key):
        return ids.setdefault(key, len(ids))

    def put(key, src, dst, target):
        i = sem_of(key)
        copy = pltpu.make_async_remote_copy(
            src_ref=src, dst_ref=dst, send_sem=send.at[i], recv_sem=recv.at[i],
            device_id=target, device_id_type=MESH,
        )
        copy.start()
        started.append(copy)

    def got(key, dst):
        i = sem_of(key)
        pltpu.make_async_remote_copy(
            src_ref=dst, dst_ref=dst, send_sem=send.at[i], recv_sem=recv.at[i],
            device_id=partner, device_id_type=MESH,
        ).wait_recv()

    l_copy = pltpu.make_async_copy(l_hbm, lbuf, lsem)
    l_copy.start()

    cross = [device(me["x"], at("y", 2), at("z", d), k) for d in (1, 2, 3)]
    greeted = [peer(a, d) for a in "xyz" for d in (1, 2, 3)] + cross + [partner]
    barrier = pltpu.get_barrier_semaphore()
    for target in greeted:
        pl.semaphore_signal(barrier, inc=1, device_id=target, device_id_type=MESH)
    pl.semaphore_wait(barrier, len(greeted))

    for d in (1, 3, 2):
        lanes = pl.ds(pl.multiple_of(at("z", d) * 512, 512), 512)
        put(("xs", d), x_ref.at[:, lanes], xs.at[me["z"]], peer("z", d))
        put(("zs", d), z_ref.at[:, lanes], zs.at[me["z"]], peer("z", d))
    lanes = pl.ds(pl.multiple_of(me["z"] * 512, 512), 512)
    xs[me["z"]] = x_ref[:, lanes]
    zs[me["z"]] = z_ref[:, lanes]

    l_copy.wait()

    def split_rows(block, carry):
        for p in range(2):
            hi, lo = split(lbuf[p, pl.ds(pl.multiple_of(block * 32, 32), 32), :])
            core, rx = lax.rem(block, 2), block // 2
            lcat[core, p, rx, :, 0:512] = hi
            lcat[core, p, rx, :, 512:1024] = hi
            lcat[core, p, rx, :, 1024:1536] = lo
        return carry

    lax.fori_loop(0, 16, split_rows, 0)

    own = (k, me["y"], me["x"], me["z"])
    for d in (1, 3, 2):
        source = lax.rem(me["z"] + 4 - d, 4)
        got(("xs", d), xs.at[source])
        got(("zs", d), zs.at[source])
    for s in range(4):
        xb[own + (slice(4 * s, 4 * s + 4), slice(None))] = xs[s]
        zb[own + (slice(2 * s, 2 * s + 2), slice(None))] = zs[s]

    full, halves = pl.ds(0, 4), (pl.ds(0, 2), pl.ds(2, 2))
    x_streams = [("x", n, xb, X_PARTS[n], ORDERS[n]) for n in range(3)]
    z_streams = [("z", n, zb, Z_PARTS[n], ORDERS[n]) for n in range(3)]

    def block(stream, core, **where):
        _, _, buf, part, _ = stream
        spot = [where.get(a, me[a]) for a in "yxz"]
        return buf.at[(core, *spot, *part)]

    def ag_direct_start(stream, phase):
        order = stream[4]
        axis, done = order[phase], {a: full for a in order[:phase]}
        for d in (1, 3, 2):
            here = block(stream, k, **done)
            put(stream[:2] + (phase, d), here, here, peer(axis, d))

    def ag_direct_wait(stream, phase):
        order = stream[4]
        axis, done = order[phase], {a: full for a in order[:phase]}
        for d in (1, 3, 2):
            got(stream[:2] + (phase, d), block(stream, k, **{axis: at(axis, 4 - d)}, **done))

    def ag_ring_part(stream, d, half=None):
        a, b, axis = stream[4]
        return {axis: at(axis, d), a: full if half is None else halves[half], b: full}

    def ag_ring_start(stream):
        axis = stream[4][2]
        for half in (0, 1):
            for d, h in ((1, half), (3, 1 - half)):
                here = block(stream, k, **ag_ring_part(stream, 0, h))
                put(stream[:2] + ("ring", d, h), here, here, peer(axis, d))
        here = block(stream, k, **ag_ring_part(stream, 0))
        put(stream[:2] + ("chip", 0), here, here, partner)

    def ag_ring_forward(stream):
        axis = stream[4][2]
        for d, h in ((1, 0), (3, 1)):
            here = block(stream, k, **ag_ring_part(stream, 4 - d, h))
            got(stream[:2] + ("ring", d, h), here)
            put(stream[:2] + ("far", d), here, here, peer(axis, d))

    def ag_ring_near(stream):
        for d, h in ((1, 1), (3, 0)):
            got(stream[:2] + ("ring", d, h), block(stream, k, **ag_ring_part(stream, 4 - d, h)))
            here = block(stream, k, **ag_ring_part(stream, 4 - d))
            put(stream[:2] + ("chip", d), here, here, partner)

    def ag_ring_far(stream):
        for d, h in ((1, 0), (3, 1)):
            got(stream[:2] + ("far", d), block(stream, k, **ag_ring_part(stream, 2, h)))
        here = block(stream, k, **ag_ring_part(stream, 2))
        put(stream[:2] + ("chip", 2), here, here, partner)

    def ag_chip_wait(stream):
        for d in (0, 1, 3, 2):
            there = block(stream, 1 - k, **ag_ring_part(stream, 0 if d == 0 else 4 - d))
            got(stream[:2] + ("chip", d), there)

    both = x_streams + z_streams
    for stream in both:
        ag_direct_start(stream, 0)
    for group in (x_streams, z_streams):
        for stream in group:
            ag_direct_wait(stream, 0)
            ag_direct_start(stream, 1)
    for group in (x_streams, z_streams):
        for stream in group:
            ag_direct_wait(stream, 1)
            ag_ring_start(stream)
    for step in (ag_ring_forward, ag_ring_near, ag_ring_far, ag_chip_wait):
        for stream in x_streams:
            step(stream)

    def row_block(index):
        return lax.rem(index, 2), index // 8, lax.rem(index // 2, 4)

    def split_factor(index, carry):
        core, y_lo, x = row_block(index)
        for y_hi in range(2):
            start = pl.multiple_of(index * 32 + y_hi * 16, 16)
            for q in range(4):
                hi, lo = split(xb[core, y_hi * 2 + y_lo, x, q])
                xcat[pl.ds(start, 16), pl.ds(q * 512, 512)] = hi
                xcat[pl.ds(512 + start, 16), pl.ds(q * 512, 512)] = lo
        return carry

    lax.fori_loop(0, 16, split_factor, 0)
    for stream in z_streams:
        ag_ring_forward(stream)

    def tile_of(t):
        return lax.rem(t, 4), t // 4

    def adjoint_tile(core, t):
        lanes = pl.ds(pl.multiple_of(t * 256, 256), 256)
        rows = lcat[core].reshape(512, 1536)
        product = dot(rows[:, :1024], xcat[:, lanes]) + dot(rows[:, 1024:], xcat[pl.ds(0, 512), lanes])
        weight0, weight1 = z_ref[0:1, lanes], z_ref[1:2, lanes]
        quarter = pl.ds(pl.multiple_of(lax.rem(t, 2) * 256, 256), 256)
        sums, out = [None, None], []
        for rx in range(8):
            y_lo, x = rx // 4, rx % 4
            piece = [product[p * 256 + rx * 32 : p * 256 + rx * 32 + 32] for p in range(2)]
            values = jnp.concatenate([xb[core, h * 2 + y_lo, x, t // 2, :, quarter] for h in range(2)], axis=0)
            for p in range(2):
                term = piece[p] * values
                sums[p] = term if sums[p] is None else sums[p] + term
            out.append((y_lo, x, piece[0] * weight0 + piece[1] * weight1))
        projected = jnp.concatenate([jnp.sum(s, axis=0, keepdims=True) for s in sums], axis=0)
        return projected, out

    chip_block = lambda buf, t: buf.at[lax.rem(t, 4), pl.ds(t // 4 * 2, 2)]

    for t in range(8):
        projected, out = adjoint_tile(1 - k, t)
        proj[t] = projected
        for y_lo, x, value in out:
            psend[t % 4, t // 4 * 2 + y_lo, x] = value
        put(("psum", t), psend.at[t % 4, pl.ds(t // 4 * 2, 2)], precv.at[t % 4, pl.ds(t // 4 * 2, 2)], partner)
    for step in (ag_ring_near, ag_ring_far):
        for stream in z_streams:
            step(stream)
    for t in range(8):
        got(("psum", t), precv.at[t % 4, pl.ds(t // 4 * 2, 2)])
        projected, out = adjoint_tile(k, t)
        proj[t] = proj[t] + projected
        for y_lo, x, value in out:
            spot = (t % 4, t // 4 * 2 + y_lo, x)
            s_buf[spot] = value + precv[spot]

    s_streams = [(n, S_PARTS[n], ORDERS[n]) for n in range(3)]

    def spot(stream, **where):
        return tuple(where[a] for a in "zyx") + stream[1]

    def rs_region(stream, d, half=None):
        a, b, e = stream[2]
        return spot(stream, **{a: at(a, d), b: full if half is None else halves[half], e: full})

    def rs_one_start(stream):
        axis = stream[2][0]
        for d, h, buf in ((1, 0, f_minus), (3, 1, f_plus)):
            where = rs_region(stream, 2, h)
            put(("s", stream[0], "far", d), s_buf.at[where], buf.at[where], peer(axis, d))
        for d, h, buf in ((1, 1, r_minus), (3, 0, r_plus)):
            where = rs_region(stream, d, h)
            put(("s", stream[0], "own", d), s_buf.at[where], buf.at[where], peer(axis, d))

    def rs_one_forward(stream):
        axis = stream[2][0]
        for d, h, buf, target in ((1, 0, f_minus, r_minus), (3, 1, f_plus, r_plus)):
            where = rs_region(stream, d, h)
            got(("s", stream[0], "far", d), buf.at[where])
            s_buf[where] = s_buf[where] + buf[where]
            put(("s", stream[0], "sum", d), s_buf.at[where], target.at[where], peer(axis, d))

    def rs_one_end(stream):
        for name, h_minus, h_plus in (("own", 1, 0), ("sum", 0, 1)):
            got(("s", stream[0], name, 1), r_minus.at[rs_region(stream, 0, h_minus)])
            got(("s", stream[0], name, 3), r_plus.at[rs_region(stream, 0, h_plus)])
        where = rs_region(stream, 0)
        s_buf[where] = s_buf[where] + r_minus[where] + r_plus[where]

    def rs_two_start(stream):
        a, b, e = stream[2]
        for d in (1, 3, 2):
            where = spot(stream, **{a: me[a], b: at(b, d), e: full})
            put(("s", stream[0], "two", d), s_buf.at[where], r_two.at[(d - 1, full) + stream[1]], peer(b, d))

    def rs_two_end(stream):
        a, b, e = stream[2]
        where = spot(stream, **{a: me[a], b: me[b], e: full})
        total = s_buf[where]
        for d in (1, 3, 2):
            got(("s", stream[0], "two", d), r_two.at[(d - 1, full) + stream[1]])
            total = total + r_two[(d - 1, full) + stream[1]]
        s_buf[where] = total

    def rs_three_start(stream):
        a, b, e = stream[2]
        for d in (1, 3, 2):
            where = spot(stream, **{a: me[a], b: me[b], e: at(e, d)})
            put(("s", stream[0], "three", d), s_buf.at[where], r_three.at[(d - 1,) + stream[1]], peer(e, d))

    def rs_three_end(stream):
        total = s_buf[spot(stream, **me)]
        for d in (1, 3, 2):
            got(("s", stream[0], "three", d), r_three.at[(d - 1,) + stream[1]])
            total = total + r_three[(d - 1,) + stream[1]]
        rows, lanes = stream[1]
        factor_out[rows, lanes] = 4.0 * (first[rows, lanes] - total)

    for stream in s_streams:
        rs_one_start(stream)

    for stream in z_streams:
        ag_chip_wait(stream)

    def split_weights(index, carry):
        core, y_lo, x = row_block(index)
        start = pl.multiple_of(index * 16, 16)
        for q in range(4):
            rows = jnp.concatenate([zb[core, h * 2 + y_lo, x, q] for h in range(2)], axis=0)
            hi, lo = split(rows)
            zcat[pl.ds(start, 16), pl.ds(q * 512, 512)] = hi
            zcat[pl.ds(256 + start, 16), pl.ds(q * 512, 512)] = lo
        return carry

    lax.fori_loop(0, 16, split_weights, 0)
    column = pl.ds(pl.multiple_of(c * 256, 256), 256)
    for source, target, depth in ((xcat, xct, 512), (zcat, zct, 256)):
        hi = source[0:depth, column].astype(F32).T.astype(BF16)
        lo = source[depth : 2 * depth, column].astype(F32).T.astype(BF16)
        target[:, 0:depth] = hi
        target[:, depth : 2 * depth] = hi
        target[:, 2 * depth : 3 * depth] = lo

    first[...] = jnp.zeros_like(first)
    weighted[...] = jnp.zeros_like(weighted)
    x_rows = [pl.ds(pl.multiple_of(base + r * 32, 32), 32) for base in (0, 512)]
    z_rows = [pl.ds(pl.multiple_of(base + r * 16, 16), 16) for base in (0, 256)]

    def gram_tile(n, carry):
        lanes = pl.ds(pl.multiple_of(n * 256, 256), 256)
        gram = dot(xct[:, 0:1024], xcat[:, lanes]) + dot(xct[:, 1024:1536], xcat[0:512, lanes])
        core_gram = dot(zct[:, 0:512], zcat[:, lanes]) + dot(zct[:, 512:768], zcat[0:256, lanes])
        for total, source, rows, value in (
            (first, xcat, x_rows, gram * core_gram),
            (weighted, zcat, z_rows, gram * gram),
        ):
            hi, lo = split(value)
            left_hi, left_lo = source[rows[0], lanes], source[rows[1], lanes]
            total[...] += dot_nt(left_hi, hi) + dot_nt(left_hi, lo) + dot_nt(left_lo, hi)
        return carry

    lax.fori_loop(0, 4, gram_tile, 0)
    for stream in s_streams:
        rs_one_forward(stream)
    lax.fori_loop(4, 8, gram_tile, 0)

    for i in range(8):
        ks[i] = weighted[2 * i : 2 * i + 2, :]
    for y, d in [(0, 1), (0, 3), (0, 2), (2, 0), (2, 1), (2, 3), (2, 2)]:
        y_to, z_to = at("y", y), at("z", d)
        put(("k", y, d), ks.at[(y_to // 2) * 4 + z_to], kb.at[c], device(me["x"], y_to, z_to, k))
    kb[c] = ks[c]

    for stream in s_streams:
        rs_one_end(stream)
        rs_two_start(stream)
    for stream in s_streams:
        rs_two_end(stream)
        rs_three_start(stream)
    for y, d in [(0, 1), (0, 3), (0, 2), (2, 0), (2, 1), (2, 3), (2, 2)]:
        y_from, z_from = at("y", y), at("z", 4 - d)
        got(("k", y, d), kb.at[(y_from // 2) * 4 + z_from])
    for i in range(8):
        core_out[:, 256 * i : 256 * i + 256] = kb[i] - proj[i]
    for stream in s_streams:
        rs_three_end(stream)
    for copy in started:
        copy.wait_send()


SEMAPHORES = 192


def on_device(cholesky_vectors, factor, core_weights):
    vmem = pl.BlockSpec(memory_space=pltpu.VMEM)
    blocks = pltpu.VMEM((4, 4, 4, 32, 256), F32)
    return pl.pallas_call(
        kernel,
        out_shape=(jax.ShapeDtypeStruct((2, 2048), F32), jax.ShapeDtypeStruct((32, 256), F32)),
        in_specs=[vmem, vmem, pl.BlockSpec(memory_space=pl.ANY)],
        out_specs=(vmem, vmem),
        scratch_shapes=[
            pltpu.VMEM((2, 512, 512), F32),
            pltpu.VMEM((2, 2, 8, 32, 1536), BF16),
            pltpu.VMEM((4, 4, 512), F32),
            pltpu.VMEM((4, 2, 512), F32),
            pltpu.VMEM((2, 4, 4, 4, 16, 512), F32),
            pltpu.VMEM((2, 4, 4, 4, 8, 512), F32),
            pltpu.VMEM((1024, 2048), BF16),
            pltpu.VMEM((512, 2048), BF16),
            pltpu.VMEM((256, 1536), BF16),
            pltpu.VMEM((256, 768), BF16),
            pltpu.VMEM((8, 2, 256), F32),
            blocks, blocks, blocks, blocks, blocks, blocks, blocks,
            pltpu.VMEM((3, 4, 32, 256), F32),
            pltpu.VMEM((3, 32, 256), F32),
            pltpu.VMEM((32, 256), F32),
            pltpu.VMEM((16, 256), F32),
            pltpu.VMEM((8, 2, 256), F32),
            pltpu.VMEM((8, 2, 256), F32),
            pltpu.SemaphoreType.DMA,
            pltpu.SemaphoreType.DMA((SEMAPHORES,)),
            pltpu.SemaphoreType.DMA((SEMAPHORES,)),
        ],
        compiler_params=pltpu.CompilerParams(
            collective_id=0, has_side_effects=True, vmem_limit_bytes=60 * 1024 * 1024
        ),
    )(factor, core_weights, cholesky_vectors)


def solution(mesh):
    placed = (P(AXES, None, None), P(AXES, None), P(AXES, None))
    return jax.shard_map(
        on_device, mesh=mesh, in_specs=placed, out_specs=(P(AXES, None), P("row", "col")), check_vma=False
    )
```

time: 1290 us -> 72.5 us (0.06)
  waiting for transfers between devices: 1210 us -> 0 us
  Pallas kernels: 0 us -> 68.8 us
  matrix products: 34.8 us -> 0 us
  local copies, waits for them, and re-layouts: 21.9 us -> 2.7 us
  between operations: 13.8 us -> 0.64 us
    reduce_scatter x1 -> x0, waiting for transfers between devices: 627 us -> none  [on_device(): summed = lax.psum_scatter(part, AXES, scatter_dimension=0, tiled=True)[0]]
    all_gather x2 -> x0, waiting for transfers between devices: 579 us -> none  [the longest x1 307 us: on_device(): x = lax.all_gather(factor, AXES, axis=0, tiled=True)]
    pallas_call x0 -> x1, Pallas kernels: none -> 68.8 us  [on_device(): pl.pallas_call(kernel, out_shape=(jax.ShapeDtypeStruct((2, 2048), F32), j...]
    dot_general x5 -> x0, matrix products: 34.8 us -> none  [the longest x4 17.8 us: dot(): lax.dot_general(a, b, (dims, ((), ())), precision=high, preferred_element...]
    unnamed x10 -> x2, local copies, waits for them, and re-layouts: 17.6 us -> 2.7 us
  transfers between devices with their start and end apart: 4 -> 0, of which waited for: 4 -> 0; matrix products, arithmetic and copies ran while one was open for 4% -> 0% of each run, Pallas kernels for 0% -> 0%
where the time goes in v2:
time: 72.5 us; the launch traced here: 72.2 us
  Pallas kernels  68.8 us (95%)
  local copies, waits for them, and re-layouts  2.7 us (4%)
    pallas_call x1, Pallas kernels, on_device(): pl.pallas_call(kernel, out_shape=(jax.ShapeDtypeStruct((2, 2048), F32), j...  68.8 us
    unnamed x2, local copies, waits for them, and re-layouts  2.7 us

profile of v2, /device:TPU:0, one launch (start us, length us, event | category | flops | bytes accessed | tf_op | source)
XLA Modules:
  0.0 72.2 jit_solution(4771585985259601720)
XLA Ops:
  0.6 68.8 %shard_map.50 = (f32[2,2048]{1,0:T(2,128)}, f32[32,256]{1,0:T(8,128)}) custom-call(f32[4,2048]{1,0:T(4,128)} %x_ref.1, f32[2,2048]{1,0:T(2,128)} %z_ref.1, f32[2,512,512]{2,1,0:T(8,128)} %l_hbm.1), custom_call_target="tpu_custom_call" | custom-call | tf_op jit(solution)/shard_map/pallas_call | solution.py:391
  69.5 1.3 %copy.7 = f32[2,2048]{1,0:T(2,128)} copy(f32[2,2048]{1,0:T(2,128)} %get-tuple-element.4) | data formatting | bytes 32768
  70.8 1.4 %copy.8 = f32[32,256]{1,0:T(8,128)} copy(f32[32,256]{1,0:T(8,128)} %get-tuple-element.5) | data formatting | bytes 65536

commit v3 on v1

v3 whole, which is shorter than its diff:
```python
import jax
import jax.numpy as jnp
from jax import lax
from jax.experimental import pallas as pl
from jax.experimental.pallas import tpu as pltpu
from jax.sharding import PartitionSpec as P

AXES = ("row", "col")
F32, BF16 = jnp.float32, jnp.bfloat16
MESH = pl.DeviceIdType.MESH

ORDERS = ("xyz", "yzx", "zxy")
X_PARTS = (
    ((pl.ds(0, 8), pl.ds(0, 128)), (pl.ds(0, 8), pl.ds(128, 128)), (pl.ds(8, 8), pl.ds(0, 256))),
    ((pl.ds(0, 8), pl.ds(0, 128)), (pl.ds(8, 8), pl.ds(0, 256)), (pl.ds(0, 8), pl.ds(128, 128))),
)
Z_PARTS = ((pl.ds(0, 8), pl.ds(0, 256)), (pl.ds(0, 8), pl.ds(256, 128)), (pl.ds(0, 8), pl.ds(384, 128)))
S_PARTS = (
    (pl.ds(0, 8), pl.ds(8, 8), pl.ds(16, 16)),
    (pl.ds(0, 8), pl.ds(8, 16), pl.ds(24, 8)),
)


def split(value):
    hi = value.astype(BF16)
    return hi, (value - hi.astype(F32)).astype(BF16)


def dot(a, b):
    return lax.dot_general(a, b, (((1,), (0,)), ((), ())), preferred_element_type=F32)


def dot_nt(a, b):
    return lax.dot_general(a, b, (((1,), (1,)), ((), ())), preferred_element_type=F32)


def kernel(
    x_hbm, z_hbm, l_hbm, core_out, factor_out,
    lbuf, lcat, xs, zs, zv, xb, zb, xcat, zcat, xct, zct, proj,
    psend, precv, s_buf, f_minus, f_plus, r_minus, r_plus, r_two, r_three,
    first, weighted, ks, kb, core_v, factor_v, local, send, recv,
):
    r, c = lax.axis_index("row"), lax.axis_index("col")
    k = lax.rem(r, 2)
    me = {
        "x": lax.rem(r // 2, 4),
        "y": (c // 4) * 2 + r // 8,
        "z": lax.rem(c, 4),
    }

    def device(x, y, z, core):
        return ((lax.rem(y, 2) * 4 + x) * 2 + core, (y // 2) * 4 + z)

    def at(axis, d):
        return lax.rem(me[axis] + d, 4)

    def peer(axis, d):
        where = dict(me)
        where[axis] = at(axis, d)
        return device(where["x"], where["y"], where["z"], k)

    partner = device(me["x"], me["y"], me["z"], 1 - k)
    send_ids, recv_ids = {}, {}

    def put(group, key, src, dst, target):
        pltpu.make_async_remote_copy(
            src_ref=src, dst_ref=dst,
            send_sem=send.at[send_ids.setdefault(group, len(send_ids))],
            recv_sem=recv.at[recv_ids.setdefault(key, len(recv_ids))],
            device_id=target, device_id_type=MESH,
        ).start()

    def got(key, whole):
        pltpu.make_async_remote_copy(
            src_ref=whole, dst_ref=whole, send_sem=send.at[0], recv_sem=recv.at[recv_ids[key]],
            device_id=partner, device_id_type=MESH,
        ).wait_recv()

    def sent(group, whole):
        pltpu.make_async_remote_copy(
            src_ref=whole, dst_ref=whole, send_sem=send.at[send_ids[group]], recv_sem=recv.at[0],
            device_id=partner, device_id_type=MESH,
        ).wait_send()

    barrier = pltpu.get_barrier_semaphore()
    greeted = [peer(a, d) for a in "xyz" for d in (1, 3, 2)] + [partner]
    for target in greeted:
        pl.semaphore_signal(barrier, inc=1, device_id=target, device_id_type=MESH)

    own_lanes = pl.ds(pl.multiple_of(me["z"] * 512, 512), 512)
    copies = [
        pltpu.make_async_copy(x_hbm.at[:, own_lanes], xs.at[me["z"]], local.at[0]),
        pltpu.make_async_copy(z_hbm.at[:, own_lanes], zs.at[me["z"]], local.at[1]),
        pltpu.make_async_copy(z_hbm, zv, local.at[2]),
        pltpu.make_async_copy(l_hbm, lbuf, local.at[3]),
    ]
    for copy in copies:
        copy.start()
    pl.semaphore_wait(barrier, len(greeted))

    for d in (1, 3, 2):
        lanes = pl.ds(pl.multiple_of(at("z", d) * 512, 512), 512)
        put("xs", "xs", x_hbm.at[:, lanes], xs.at[me["z"]], peer("z", d))
    for d in (1, 3, 2):
        lanes = pl.ds(pl.multiple_of(at("z", d) * 512, 512), 512)
        put("zs", "zs", z_hbm.at[:, lanes], zs.at[me["z"]], peer("z", d))

    for copy in copies:
        copy.wait()

    def split_rows(block, carry):
        for p in range(2):
            hi, lo = split(lbuf[p, pl.ds(pl.multiple_of(block * 32, 32), 32), :])
            core, rx = lax.rem(block, 2), block // 2
            lcat[core, p, rx, :, 0:512] = hi
            lcat[core, p, rx, :, 512:1024] = hi
            lcat[core, p, rx, :, 1024:1536] = lo
        return carry

    full, halves = pl.ds(0, 4), (pl.ds(0, 2), pl.ds(2, 2))
    spot = (me["y"], me["x"], me["z"])
    got("xs", xs.at[pl.ds(0, 3)])
    for h in range(2):
        for e in range(2):
            for s in range(4):
                lanes = slice(e * 256 + h * 128, e * 256 + h * 128 + 128)
                xb[(k, h) + spot + (slice(4 * s, 4 * s + 4), slice(e * 128, e * 128 + 128))] = xs[s, :, lanes]

    def streams(name, buf, lead, parts):
        return [(name, n, buf, lead, parts[n], ORDERS[n]) for n in range(3)]

    x_streams = [streams("x%d" % h, xb, (h,), X_PARTS[h]) for h in range(2)]
    z_streams = streams("z", zb, (), Z_PARTS)

    def block(stream, core, **where):
        _, _, buf, lead, part, _ = stream
        return buf.at[(core,) + lead + tuple(where.get(a, me[a]) for a in "yxz") + part]

    def whole(group, *counts):
        _, _, buf, lead, _, _ = group[0]
        return buf.at[(0,) + lead + tuple(pl.ds(0, n) for n in counts)]

    def parts_of(stream, *counts):
        _, _, buf, lead, part, _ = stream
        return buf.at[(0,) + lead + tuple(pl.ds(0, n) for n in counts) + part]

    def ag_direct_start(group, phase):
        for stream in group:
            name, order = stream[0], stream[5]
            axis, done = order[phase], {a: full for a in order[:phase]}
            here = block(stream, k, **done)
            for d in (1, 3, 2):
                put((name, phase), (name, phase), here, here, peer(axis, d))

    def ag_direct_wait(group, phase):
        got((group[0][0], phase), whole(group, 1, 3, 4 if phase else 1))

    def ag_ring_part(stream, d, half=None):
        a, b, axis = stream[5]
        return {axis: at(axis, d), a: full if half is None else halves[half], b: full}

    def ag_ring_start(group):
        for half in (0, 1):
            for stream in group:
                axis = stream[5][2]
                for d, h in ((1, half), (3, 1 - half)):
                    here = block(stream, k, **ag_ring_part(stream, 0, h))
                    put((stream[0], "ring"), stream[:2] + ("near", half), here, here, peer(axis, d))
        for stream in group:
            here = block(stream, k, **ag_ring_part(stream, 0))
            put((stream[0], "chip"), (stream[0], "chip"), here, here, partner)

    def ag_ring_forward(group):
        for stream in group:
            axis = stream[5][2]
            got(stream[:2] + ("near", 0), parts_of(stream, 1, 4, 4))
            for d, h in ((1, 0), (3, 1)):
                here = block(stream, k, **ag_ring_part(stream, 4 - d, h))
                put((stream[0], "ring"), stream[:2] + ("far",), here, here, peer(axis, d))

    def ag_ring_near(group):
        for stream in group:
            got(stream[:2] + ("near", 1), parts_of(stream, 1, 4, 4))
            for d in (1, 3):
                here = block(stream, k, **ag_ring_part(stream, d))
                put((stream[0], "chip"), (stream[0], "chip"), here, here, partner)

    def ag_ring_far(group):
        for stream in group:
            got(stream[:2] + ("far",), parts_of(stream, 1, 4, 4))
            here = block(stream, k, **ag_ring_part(stream, 2))
            put((stream[0], "chip"), (stream[0], "chip"), here, here, partner)

    def ag_chip_wait(group):
        got((group[0][0], "chip"), whole(group, 4, 4, 4))

    def ag_sent(group):
        name = group[0][0]
        for phase, counts in ((0, (1, 3, 1)), (1, (1, 3, 4)), ("ring", (3, 4, 4)), ("chip", (4, 4, 4))):
            sent((name, phase), whole(group, *counts))

    ag_direct_start(x_streams[0], 0)
    ag_direct_start(x_streams[1], 0)
    got("zs", zs.at[pl.ds(0, 3)])
    for h in range(2):
        for e in range(2):
            for s in range(4):
                lanes = slice(e * 256 + h * 128, e * 256 + h * 128 + 128)
                to = slice((2 * h + e) * 128, (2 * h + e) * 128 + 128)
                zb[(k,) + spot + (slice(2 * s, 2 * s + 2), to)] = zs[s, :, lanes]
    ag_direct_start(z_streams, 0)
    lax.fori_loop(0, 8, split_rows, 0)
    for group in x_streams:
        ag_direct_wait(group, 0)
        ag_direct_start(group, 1)
    lax.fori_loop(8, 16, split_rows, 0)
    for group in x_streams:
        ag_direct_wait(group, 1)
        ag_ring_start(group)
    ag_direct_wait(z_streams, 0)
    ag_direct_start(z_streams, 1)
    ag_ring_forward(x_streams[0])
    ag_ring_near(x_streams[0])
    ag_direct_wait(z_streams, 1)
    ag_ring_far(x_streams[0])
    ag_ring_start(z_streams)
    ag_ring_forward(x_streams[1])
    ag_chip_wait(x_streams[0])

    def row_block(index):
        return lax.rem(index, 2), index // 8, lax.rem(index // 2, 4)

    def split_factor(h):
        def body(index, carry):
            core, y_lo, x = row_block(index)
            for y_hi in range(2):
                start = pl.multiple_of(index * 32 + y_hi * 16, 16)
                for q in range(4):
                    hi, lo = split(xb[core, h, y_hi * 2 + y_lo, x, q])
                    xcat[h, pl.ds(start, 16), q * 256 : q * 256 + 256] = hi
                    xcat[h, pl.ds(512 + start, 16), q * 256 : q * 256 + 256] = lo
            return carry

        lax.fori_loop(0, 16, body, 0)

    def adjoint_chunk(core, h, target, fresh):
        for q in range(4):
            lanes = slice(q * 256, q * 256 + 256)
            rows = lcat[core].reshape(512, 1536)
            product = dot(rows[:, :1024], xcat[h, :, lanes]) + dot(rows[:, 1024:], xcat[h, 0:512, lanes])
            starts = [(2 * q + e) * 256 + h * 128 for e in range(2)]
            weights = [
                jnp.concatenate([zv[p : p + 1, at_ : at_ + 128] for at_ in starts], axis=1) for p in range(2)
            ]
            sums = [None, None]
            for rx in range(8):
                y_lo, x = rx // 4, rx % 4
                piece = [product[p * 256 + rx * 32 : p * 256 + rx * 32 + 32] for p in range(2)]
                values = jnp.concatenate([xb[core, h, i * 2 + y_lo, x, q] for i in range(2)], axis=0)
                for p in range(2):
                    term = piece[p] * values
                    sums[p] = term if sums[p] is None else sums[p] + term
                value = piece[0] * weights[0] + piece[1] * weights[1]
                for e in range(2):
                    y, z = q // 2 * 2 + y_lo, (2 * q + e) % 4
                    target[h, z, y, x] = value[:, e * 128 : e * 128 + 128]
            projected = jnp.concatenate([jnp.sum(s, axis=0, keepdims=True) for s in sums], axis=0)
            half = slice(h * 128, h * 128 + 128)
            for e in range(2):
                part = projected[:, e * 128 : e * 128 + 128]
                proj[2 * q + e, :, half] = part if fresh else proj[2 * q + e, :, half] + part

    s_streams = [[("s%d" % h, n, h, S_PARTS[h][n], ORDERS[n]) for n in range(3)] for h in range(2)]

    def place(stream, **where):
        return (stream[2],) + tuple(where[a] for a in "zyx") + (stream[3],)

    def rs_region(stream, d, half=None):
        a, b, e = stream[4]
        return place(stream, **{a: at(a, d), b: full if half is None else halves[half], e: full})

    def rs_count(stream, *counts):
        return s_buf.at[(stream[2],) + tuple(pl.ds(0, n) for n in counts) + (stream[3],)]

    def rs_whole(group, *counts):
        return s_buf.at[(group[0][2],) + tuple(pl.ds(0, n) for n in counts)]

    def rs_one_start(group):
        for stream in group:
            axis = stream[4][0]
            for d, h, buf in ((1, 0, f_minus), (3, 1, f_plus)):
                where = rs_region(stream, 2, h)
                put((stream[0], "one"), stream[:2] + ("far",), s_buf.at[where], buf.at[where], peer(axis, d))
        for stream in group:
            axis = stream[4][0]
            for d, h, buf in ((1, 1, r_minus), (3, 0, r_plus)):
                where = rs_region(stream, d, h)
                put((stream[0], "one"), stream[:2] + ("near",), s_buf.at[where], buf.at[where], peer(axis, d))

    def rs_one_forward(group):
        for stream in group:
            axis = stream[4][0]
            got(stream[:2] + ("far",), rs_count(stream, 1, 4, 4))
            for d, h, buf, target in ((1, 0, f_minus, r_minus), (3, 1, f_plus, r_plus)):
                where = rs_region(stream, d, h)
                s_buf[where] = s_buf[where] + buf[where]
                put((stream[0], "one"), stream[:2] + ("near",), s_buf.at[where], target.at[where], peer(axis, d))

    def rs_one_end(group):
        for stream in group:
            got(stream[:2] + ("near",), rs_count(stream, 2, 4, 4))
            where = rs_region(stream, 0)
            s_buf[where] = s_buf[where] + r_minus[where] + r_plus[where]
            a, b, e = stream[4]
            for d in (1, 3, 2):
                where = place(stream, **{a: me[a], b: at(b, d), e: full})
                put(
                    (stream[0], "two"), stream[:2] + ("two",),
                    s_buf.at[where], r_two.at[stream[2], d - 1, :, stream[3]], peer(b, d),
                )

    def rs_two_end(group):
        for stream in group:
            a, b, e = stream[4]
            got(stream[:2] + ("two",), rs_count(stream, 1, 3, 4))
            where = place(stream, **{a: me[a], b: me[b], e: full})
            total = s_buf[where]
            for d in (1, 3, 2):
                total = total + r_two[stream[2], d - 1, :, stream[3]]
            s_buf[where] = total
            for d in (1, 3, 2):
                where = place(stream, **{a: me[a], b: me[b], e: at(e, d)})
                put(
                    (stream[0], "three"), (stream[0], "three"),
                    s_buf.at[where], r_three.at[stream[2], d - 1, stream[3]], peer(e, d),
                )

    def rs_three_end(group):
        h = group[0][2]
        got((group[0][0], "three"), rs_whole(group, 1, 1, 3))
        total = s_buf[h, me["z"], me["y"], me["x"]]
        for d in (1, 3, 2):
            total = total + r_three[h, d - 1]
        half = slice(h * 128, h * 128 + 128)
        factor_v[:, half] = 4.0 * (first[:, half] - total)

    def rs_sent(group):
        for name, counts in (("one", (3, 4, 4)), ("two", (1, 3, 4)), ("three", (1, 1, 3))):
            sent((group[0][0], name), rs_whole(group, *counts))

    def partner_start(h):
        put("sum", ("sum", h), psend.at[h], precv.at[h], partner)

    def partner_end(h):
        got(("sum", h), precv.at[h])
        for z in range(4):
            s_buf[h, z] = s_buf[h, z] + precv[h, z]

    split_factor(0)
    adjoint_chunk(1 - k, 0, psend, True)
    partner_start(0)
    ag_ring_near(x_streams[1])
    adjoint_chunk(k, 0, s_buf, False)
    partner_end(0)
    rs_one_start(s_streams[0])
    ag_ring_far(x_streams[1])
    ag_ring_forward(z_streams)
    ag_chip_wait(x_streams[1])
    split_factor(1)
    adjoint_chunk(1 - k, 1, psend, True)
    partner_start(1)
    rs_one_forward(s_streams[0])
    ag_ring_near(z_streams)
    adjoint_chunk(k, 1, s_buf, False)
    partner_end(1)
    rs_one_start(s_streams[1])
    ag_ring_far(z_streams)
    rs_one_end(s_streams[0])

    def split_weights(index, carry):
        core, y_lo, x = row_block(index)
        start = pl.multiple_of(index * 16, 16)
        for h in range(2):
            for q in range(4):
                rows = jnp.concatenate(
                    [zb[core, i * 2 + y_lo, x, q, :, h * 256 : h * 256 + 256] for i in range(2)], axis=0
                )
                hi, lo = split(rows)
                zcat[h, pl.ds(start, 16), q * 256 : q * 256 + 256] = hi
                zcat[h, pl.ds(256 + start, 16), q * 256 : q * 256 + 256] = lo
        return carry

    column = pl.ds(pl.multiple_of(c * 128, 128), 128)

    def transpose(source, target, depth):
        for h in range(2):
            rows = slice(h * 128, h * 128 + 128)
            hi = source[h, 0:depth, column].astype(F32).T.astype(BF16)
            lo = source[h, depth : 2 * depth, column].astype(F32).T.astype(BF16)
            target[rows, 0:depth] = hi
            target[rows, depth : 2 * depth] = hi
            target[rows, 2 * depth : 3 * depth] = lo

    transpose(xcat, xct, 512)
    ag_chip_wait(z_streams)
    lax.fori_loop(0, 16, split_weights, 0)
    rs_one_forward(s_streams[1])
    transpose(zcat, zct, 256)

    first[...] = jnp.zeros_like(first)
    weighted[...] = jnp.zeros_like(weighted)
    x_rows = [pl.ds(pl.multiple_of(base + r * 32, 32), 32) for base in (0, 512)]
    z_rows = [pl.ds(pl.multiple_of(base + r * 16, 16), 16) for base in (0, 256)]

    def gram_tile(h, q):
        lanes = slice(q * 256, q * 256 + 256)
        gram = dot(xct[:, 0:1024], xcat[h, :, lanes]) + dot(xct[:, 1024:1536], xcat[h, 0:512, lanes])
        core_gram = dot(zct[:, 0:512], zcat[h, :, lanes]) + dot(zct[:, 512:768], zcat[h, 0:256, lanes])
        for total, source, rows, value in (
            (first, xcat, x_rows, gram * core_gram),
            (weighted, zcat, z_rows, gram * gram),
        ):
            hi, lo = split(value)
            left_hi, left_lo = source[h, rows[0], lanes], source[h, rows[1], lanes]
            total[...] += dot_nt(left_hi, hi) + dot_nt(left_hi, lo) + dot_nt(left_lo, hi)

    gram_tile(0, 0)
    gram_tile(0, 1)
    rs_two_end(s_streams[0])
    gram_tile(0, 2)
    gram_tile(0, 3)
    rs_one_end(s_streams[1])
    for q in range(4):
        gram_tile(1, q)
    rs_two_end(s_streams[1])

    for i in range(8):
        ks[i] = weighted[2 * i : 2 * i + 2, :]
    for y, d in [(0, 1), (0, 3), (0, 2), (2, 0), (2, 1), (2, 3), (2, 2)]:
        y_to, z_to = at("y", y), at("z", d)
        put("k", "k", ks.at[(y_to // 2) * 4 + z_to], kb.at[c], device(me["x"], y_to, z_to, k))
    kb[c] = ks[c]
    rs_three_end(s_streams[0])
    rs_three_end(s_streams[1])
    factor_copy = pltpu.make_async_copy(factor_v, factor_out, local.at[0])
    factor_copy.start()
    got("k", kb.at[pl.ds(0, 7)])
    for i in range(8):
        core_v[:, 256 * i : 256 * i + 256] = kb[i] - proj[i]
    core_copy = pltpu.make_async_copy(core_v, core_out, local.at[1])
    core_copy.start()

    sent("xs", xs.at[pl.ds(0, 3)])
    sent("zs", zs.at[pl.ds(0, 3)])
    for group in x_streams + [z_streams]:
        ag_sent(group)
    for group in s_streams:
        rs_sent(group)
    sent("sum", psend)
    sent("k", ks.at[pl.ds(0, 7)])
    factor_copy.wait()
    core_copy.wait()
    assert len(send_ids) <= SENDS and len(recv_ids) <= RECVS


SENDS, RECVS = 22, 61


def write_out(core_ref, factor_ref, core_out, factor_out):
    core_out[...] = core_ref[...]
    factor_out[...] = factor_ref[...]


def on_device(cholesky_vectors, factor, core_weights):
    anywhere, vmem = pl.BlockSpec(memory_space=pl.ANY), pl.BlockSpec(memory_space=pltpu.VMEM)
    blocks = pltpu.VMEM((2, 4, 4, 4, 32, 128), F32)
    shapes = (jax.ShapeDtypeStruct((2, 2048), F32), jax.ShapeDtypeStruct((32, 256), F32))
    results = pl.pallas_call(
        kernel,
        out_shape=shapes,
        in_specs=[anywhere] * 3,
        out_specs=(anywhere, anywhere),
        scratch_shapes=[
            pltpu.VMEM((2, 512, 512), F32),
            pltpu.VMEM((2, 2, 8, 32, 1536), BF16),
            pltpu.VMEM((4, 4, 512), F32),
            pltpu.VMEM((4, 2, 512), F32),
            pltpu.VMEM((2, 2048), F32),
            pltpu.VMEM((2, 2, 4, 4, 4, 16, 256), F32),
            pltpu.VMEM((2, 4, 4, 4, 8, 512), F32),
            pltpu.VMEM((2, 1024, 1024), BF16),
            pltpu.VMEM((2, 512, 1024), BF16),
            pltpu.VMEM((256, 1536), BF16),
            pltpu.VMEM((256, 768), BF16),
            pltpu.VMEM((8, 2, 256), F32),
            blocks, blocks, blocks, blocks, blocks, blocks, blocks,
            pltpu.VMEM((2, 3, 4, 32, 128), F32),
            pltpu.VMEM((2, 3, 32, 128), F32),
            pltpu.VMEM((32, 256), F32),
            pltpu.VMEM((16, 256), F32),
            pltpu.VMEM((8, 2, 256), F32),
            pltpu.VMEM((8, 2, 256), F32),
            pltpu.VMEM((2, 2048), F32),
            pltpu.VMEM((32, 256), F32),
            pltpu.SemaphoreType.DMA((4,)),
            pltpu.SemaphoreType.DMA((SENDS,)),
            pltpu.SemaphoreType.DMA((RECVS,)),
        ],
        compiler_params=pltpu.CompilerParams(
            collective_id=0, has_side_effects=True, vmem_limit_bytes=60 * 1024 * 1024
        ),
    )(factor, core_weights, cholesky_vectors)
    return pl.pallas_call(write_out, out_shape=shapes, in_specs=[vmem, vmem], out_specs=(vmem, vmem))(*results)


def solution(mesh):
    placed = (P(AXES, None, None), P(AXES, None), P(AXES, None))
    return jax.shard_map(
        on_device, mesh=mesh, in_specs=placed, out_specs=(P(AXES, None), P("row", "col")), check_vma=False
    )
```

time: 1290 us -> 60.1 us (0.05)
  waiting for transfers between devices: 1210 us -> 0 us
  Pallas kernels: 0 us -> 59.2 us
  matrix products: 34.8 us -> 0 us
  local copies, waits for them, and re-layouts: 21.9 us -> 0 us
  between operations: 13.8 us -> 0.64 us
    reduce_scatter x1 -> x0, waiting for transfers between devices: 627 us -> none  [on_device(): summed = lax.psum_scatter(part, AXES, scatter_dimension=0, tiled=True)[0]]
    all_gather x2 -> x0, waiting for transfers between devices: 579 us -> none  [the longest x1 307 us: on_device(): x = lax.all_gather(factor, AXES, axis=0, tiled=True)]
    pallas_call x0 -> x2, Pallas kernels: none -> 59.2 us  [the longest x1 57.8 us: on_device(): pl.pallas_call(kernel, out_shape=shapes, in_specs=[anywhere] * 3, out_spe...]
    dot_general x5 -> x0, matrix products: 34.8 us -> none  [the longest x4 17.8 us: dot(): lax.dot_general(a, b, (dims, ((), ())), precision=high, preferred_element...]
    unnamed x10 -> x0, local copies, waits for them, and re-layouts: 17.6 us -> none
  transfers between devices with their start and end apart: 4 -> 0, of which waited for: 4 -> 0; matrix products, arithmetic and copies ran while one was open for 4% -> 0% of each run, Pallas kernels for 0% -> 0%
where the time goes in v3:
time: 60.1 us; the launch traced here: 59.9 us
  Pallas kernels  59.2 us (99%)
  between operations  0.64 us (1%)
    pallas_call x1, Pallas kernels, on_device(): pl.pallas_call(kernel, out_shape=shapes, in_specs=[anywhere] * 3, out_spe...  57.8 us
    pallas_call x1, Pallas kernels, on_device(): pl.pallas_call(write_out, out_shape=shapes, in_specs=[vmem, vmem], out_sp...  1.4 us

profile of v3, /device:TPU:0, one launch (start us, length us, event | category | flops | bytes accessed | tf_op | source)
XLA Modules:
  0.0 59.9 jit_solution(11546503614401106704)
XLA Ops:
  0.6 57.8 %shard_map.50 = (f32[2,2048]{1,0:T(2,128)}, f32[32,256]{1,0:T(8,128)}) custom-call(f32[4,2048]{1,0:T(4,128)} %x_hbm.1, f32[2,2048]{1,0:T(2,128)} %z_hbm.1, f32[2,512,512]{2,1,0:T(8,128)} %l_hbm.1), custom_call_target="tpu_custom_call" | custom-call | tf_op jit(solution)/shard_map/pallas_call | solution.py:478
  58.5 1.4 %shard_map.51 = (f32[2,2048]{1,0:T(2,128)}, f32[32,256]{1,0:T(8,128)}) custom-call(f32[2,2048]{1,0:T(2,128)} %get-tuple-element.4.core_ref, f32[32,256]{1,0:T(8,128)} %get-tuple-element.5.factor_ref), custom_call_target="tpu_custom_call" | custom-call | tf_op jit(solution)/shard_map/pallas_call | solution.py:513

commit v4 on v3

--- a/solution.py
+++ b/solution.py
@@ -9,12 +9,12 @@
 F32, BF16 = jnp.float32, jnp.bfloat16
 MESH = pl.DeviceIdType.MESH
 
+GATHER_ORDERS = {"x": ("xy", "yx"), "z": ("xyz", "yxz")}
+GATHER_PARTS = {
+    "x": ((pl.ds(0, 8), pl.ds(0, 1024)), (pl.ds(8, 8), pl.ds(0, 1024))),
+    "z": ((pl.ds(0, 8), pl.ds(0, 256)), (pl.ds(0, 8), pl.ds(256, 256))),
+}
 ORDERS = ("xyz", "yzx", "zxy")
-X_PARTS = (
-    ((pl.ds(0, 8), pl.ds(0, 128)), (pl.ds(0, 8), pl.ds(128, 128)), (pl.ds(8, 8), pl.ds(0, 256))),
-    ((pl.ds(0, 8), pl.ds(0, 128)), (pl.ds(8, 8), pl.ds(0, 256)), (pl.ds(0, 8), pl.ds(128, 128))),
-)
-Z_PARTS = ((pl.ds(0, 8), pl.ds(0, 256)), (pl.ds(0, 8), pl.ds(256, 128)), (pl.ds(0, 8), pl.ds(384, 128)))
 S_PARTS = (
     (pl.ds(0, 8), pl.ds(8, 8), pl.ds(16, 16)),
     (pl.ds(0, 8), pl.ds(8, 16), pl.ds(24, 8)),
@@ -37,7 +37,7 @@
 def kernel(
     x_hbm, z_hbm, l_hbm, core_out, factor_out,
     lbuf, lcat, xs, zs, zv, xb, zb, xcat, zcat, xct, zct, proj,
-    psend, precv, s_buf, f_minus, f_plus, r_minus, r_plus, r_two, r_three,
+    psend, precv, s_buf, f_minus, f_plus, r_minus, r_plus, r_two,
     first, weighted, ks, kb, core_v, factor_v, local, send, recv,
 ):
     r, c = lax.axis_index("row"), lax.axis_index("col")
@@ -89,7 +89,7 @@
 
     own_lanes = pl.ds(pl.multiple_of(me["z"] * 512, 512), 512)
     copies = [
-        pltpu.make_async_copy(x_hbm.at[:, own_lanes], xs.at[me["z"]], local.at[0]),
+        pltpu.make_async_copy(x_hbm, xs.at[me["z"]], local.at[0]),
         pltpu.make_async_copy(z_hbm.at[:, own_lanes], zs.at[me["z"]], local.at[1]),
         pltpu.make_async_copy(z_hbm, zv, local.at[2]),
         pltpu.make_async_copy(l_hbm, lbuf, local.at[3]),
@@ -99,8 +99,7 @@
     pl.semaphore_wait(barrier, len(greeted))
 
     for d in (1, 3, 2):
-        lanes = pl.ds(pl.multiple_of(at("z", d) * 512, 512), 512)
-        put("xs", "xs", x_hbm.at[:, lanes], xs.at[me["z"]], peer("z", d))
+        put("xs", "xs", x_hbm, xs.at[me["z"]], peer("z", d))
     for d in (1, 3, 2):
         lanes = pl.ds(pl.multiple_of(at("z", d) * 512, 512), 512)
         put("zs", "zs", z_hbm.at[:, lanes], zs.at[me["z"]], peer("z", d))
@@ -118,31 +117,25 @@
         return carry
 
     full, halves = pl.ds(0, 4), (pl.ds(0, 2), pl.ds(2, 2))
-    spot = (me["y"], me["x"], me["z"])
-    got("xs", xs.at[pl.ds(0, 3)])
-    for h in range(2):
-        for e in range(2):
-            for s in range(4):
-                lanes = slice(e * 256 + h * 128, e * 256 + h * 128 + 128)
-                xb[(k, h) + spot + (slice(4 * s, 4 * s + 4), slice(e * 128, e * 128 + 128))] = xs[s, :, lanes]
-
-    def streams(name, buf, lead, parts):
-        return [(name, n, buf, lead, parts[n], ORDERS[n]) for n in range(3)]
-
-    x_streams = [streams("x%d" % h, xb, (h,), X_PARTS[h]) for h in range(2)]
-    z_streams = streams("z", zb, (), Z_PARTS)
+
+    def streams(name, buf, lead, dims):
+        kind = name[0]
+        return [(name, n, buf, lead, GATHER_PARTS[kind][n], GATHER_ORDERS[kind][n], dims) for n in range(2)]
+
+    x_streams = [streams("x%d" % h, xb, (h,), "yx") for h in range(2)]
+    z_streams = streams("z", zb, (), "yxz")
 
     def block(stream, core, **where):
-        _, _, buf, lead, part, _ = stream
-        return buf.at[(core,) + lead + tuple(where.get(a, me[a]) for a in "yxz") + part]
+        _, _, buf, lead, part, _, dims = stream
+        return buf.at[(core,) + lead + tuple(where.get(a, me[a]) for a in dims) + part]
 
     def whole(group, *counts):
-        _, _, buf, lead, _, _ = group[0]
-        return buf.at[(0,) + lead + tuple(pl.ds(0, n) for n in counts)]
+        _, _, buf, lead, _, _, dims = group[0]
+        return buf.at[(0,) + lead + tuple(pl.ds(0, n) for n in counts[-len(dims) :])]
 
     def parts_of(stream, *counts):
-        _, _, buf, lead, part, _ = stream
-        return buf.at[(0,) + lead + tuple(pl.ds(0, n) for n in counts) + part]
+        _, _, buf, lead, part, _, dims = stream
+        return buf.at[(0,) + lead + tuple(pl.ds(0, n) for n in counts[-len(dims) :]) + part]
 
     def ag_direct_start(group, phase):
         for stream in group:
@@ -156,13 +149,17 @@
         got((group[0][0], phase), whole(group, 1, 3, 4 if phase else 1))
 
     def ag_ring_part(stream, d, half=None):
-        a, b, axis = stream[5]
-        return {axis: at(axis, d), a: full if half is None else halves[half], b: full}
+        order = stream[5]
+        where = {a: full for a in order[:-1]}
+        if half is not None:
+            where[order[0]] = halves[half]
+        where[order[-1]] = at(order[-1], d)
+        return where
 
     def ag_ring_start(group):
         for half in (0, 1):
             for stream in group:
-                axis = stream[5][2]
+                axis = stream[5][-1]
                 for d, h in ((1, half), (3, 1 - half)):
                     here = block(stream, k, **ag_ring_part(stream, 0, h))
                     put((stream[0], "ring"), stream[:2] + ("near", half), here, here, peer(axis, d))
@@ -170,60 +167,69 @@
             here = block(stream, k, **ag_ring_part(stream, 0))
             put((stream[0], "chip"), (stream[0], "chip"), here, here, partner)
 
+    def ring_counts(stream, n):
+        return (1, n, 4) if len(stream[5]) == 2 else (n, 4, 4)
+
     def ag_ring_forward(group):
         for stream in group:
-            axis = stream[5][2]
-            got(stream[:2] + ("near", 0), parts_of(stream, 1, 4, 4))
+            axis = stream[5][-1]
+            got(stream[:2] + ("near", 0), parts_of(stream, *ring_counts(stream, 1)))
             for d, h in ((1, 0), (3, 1)):
                 here = block(stream, k, **ag_ring_part(stream, 4 - d, h))
                 put((stream[0], "ring"), stream[:2] + ("far",), here, here, peer(axis, d))
 
     def ag_ring_near(group):
         for stream in group:
-            got(stream[:2] + ("near", 1), parts_of(stream, 1, 4, 4))
+            got(stream[:2] + ("near", 1), parts_of(stream, *ring_counts(stream, 1)))
             for d in (1, 3):
                 here = block(stream, k, **ag_ring_part(stream, d))
                 put((stream[0], "chip"), (stream[0], "chip"), here, here, partner)
 
     def ag_ring_far(group):
         for stream in group:
-            got(stream[:2] + ("far",), parts_of(stream, 1, 4, 4))
+            got(stream[:2] + ("far",), parts_of(stream, *ring_counts(stream, 1)))
             here = block(stream, k, **ag_ring_part(stream, 2))
             put((stream[0], "chip"), (stream[0], "chip"), here, here, partner)
 
     def ag_chip_wait(group):
-        got((group[0][0], "chip"), whole(group, 4, 4, 4))
+        got((group[0][0], "chip"), whole(group, *ring_counts(group[0], 4)))
 
     def ag_sent(group):
-        name = group[0][0]
-        for phase, counts in ((0, (1, 3, 1)), (1, (1, 3, 4)), ("ring", (3, 4, 4)), ("chip", (4, 4, 4))):
-            sent((name, phase), whole(group, *counts))
-
-    ag_direct_start(x_streams[0], 0)
-    ag_direct_start(x_streams[1], 0)
+        name, order = group[0][0], group[0][5]
+        sent((name, 0), whole(group, 1, 3, 1))
+        if len(order) == 3:
+            sent((name, 1), whole(group, 1, 3, 4))
+        sent((name, "ring"), whole(group, *ring_counts(group[0], 3)))
+        sent((name, "chip"), whole(group, *ring_counts(group[0], 4)))
+
+    got("xs", xs.at[pl.ds(0, 3)])
+    for h in range(2):
+        for i in range(8):
+            for s in range(4):
+                lanes = slice(i * 256 + h * 128, i * 256 + h * 128 + 128)
+                xb[k, h, me["y"], me["x"], 4 * s : 4 * s + 4, i * 128 : i * 128 + 128] = xs[s, :, lanes]
+        ag_direct_start(x_streams[h], 0)
     got("zs", zs.at[pl.ds(0, 3)])
     for h in range(2):
         for e in range(2):
             for s in range(4):
                 lanes = slice(e * 256 + h * 128, e * 256 + h * 128 + 128)
                 to = slice((2 * h + e) * 128, (2 * h + e) * 128 + 128)
-                zb[(k,) + spot + (slice(2 * s, 2 * s + 2), to)] = zs[s, :, lanes]
+                zb[k, me["y"], me["x"], me["z"], 2 * s : 2 * s + 2, to] = zs[s, :, lanes]
     ag_direct_start(z_streams, 0)
     lax.fori_loop(0, 8, split_rows, 0)
-    for group in x_streams:
-        ag_direct_wait(group, 0)
-        ag_direct_start(group, 1)
-    lax.fori_loop(8, 16, split_rows, 0)
-    for group in x_streams:
-        ag_direct_wait(group, 1)
-        ag_ring_start(group)
+    ag_direct_wait(x_streams[0], 0)
+    ag_ring_start(x_streams[0])
     ag_direct_wait(z_streams, 0)
     ag_direct_start(z_streams, 1)
+    ag_direct_wait(x_streams[1], 0)
+    ag_ring_start(x_streams[1])
+    lax.fori_loop(8, 16, split_rows, 0)
     ag_ring_forward(x_streams[0])
     ag_ring_near(x_streams[0])
     ag_direct_wait(z_streams, 1)
+    ag_ring_start(z_streams)
     ag_ring_far(x_streams[0])
-    ag_ring_start(z_streams)
     ag_ring_forward(x_streams[1])
     ag_chip_wait(x_streams[0])
 
@@ -236,7 +242,7 @@
             for y_hi in range(2):
                 start = pl.multiple_of(index * 32 + y_hi * 16, 16)
                 for q in range(4):
-                    hi, lo = split(xb[core, h, y_hi * 2 + y_lo, x, q])
+                    hi, lo = split(xb[core, h, y_hi * 2 + y_lo, x, :, q * 256 : q * 256 + 256])
                     xcat[h, pl.ds(start, 16), q * 256 : q * 256 + 256] = hi
                     xcat[h, pl.ds(512 + start, 16), q * 256 : q * 256 + 256] = lo
             return carry
@@ -256,7 +262,7 @@
             for rx in range(8):
                 y_lo, x = rx // 4, rx % 4
                 piece = [product[p * 256 + rx * 32 : p * 256 + rx * 32 + 32] for p in range(2)]
-                values = jnp.concatenate([xb[core, h, i * 2 + y_lo, x, q] for i in range(2)], axis=0)
+                values = jnp.concatenate([xb[core, h, i * 2 + y_lo, x, :, lanes] for i in range(2)], axis=0)
                 for p in range(2):
                     term = piece[p] * values
                     sums[p] = term if sums[p] is None else sums[p] + term
@@ -312,41 +318,26 @@
             where = rs_region(stream, 0)
             s_buf[where] = s_buf[where] + r_minus[where] + r_plus[where]
             a, b, e = stream[4]
-            for d in (1, 3, 2):
-                where = place(stream, **{a: me[a], b: at(b, d), e: full})
+            for db, de in PLANE:
+                where = place(stream, **{a: me[a], b: at(b, db), e: at(e, de)})
+                to = {a: me[a], b: at(b, db), e: at(e, de)}
                 put(
-                    (stream[0], "two"), stream[:2] + ("two",),
-                    s_buf.at[where], r_two.at[stream[2], d - 1, :, stream[3]], peer(b, d),
+                    (stream[0], "two"), (stream[0], "two"),
+                    s_buf.at[where], r_two.at[stream[2], db * 4 + de - 1, stream[3]], device(**to, core=k),
                 )
 
     def rs_two_end(group):
-        for stream in group:
-            a, b, e = stream[4]
-            got(stream[:2] + ("two",), rs_count(stream, 1, 3, 4))
-            where = place(stream, **{a: me[a], b: me[b], e: full})
-            total = s_buf[where]
-            for d in (1, 3, 2):
-                total = total + r_two[stream[2], d - 1, :, stream[3]]
-            s_buf[where] = total
-            for d in (1, 3, 2):
-                where = place(stream, **{a: me[a], b: me[b], e: at(e, d)})
-                put(
-                    (stream[0], "three"), (stream[0], "three"),
-                    s_buf.at[where], r_three.at[stream[2], d - 1, stream[3]], peer(e, d),
-                )
-
-    def rs_three_end(group):
         h = group[0][2]
-        got((group[0][0], "three"), rs_whole(group, 1, 1, 3))
+        got((group[0][0], "two"), r_two.at[h])
         total = s_buf[h, me["z"], me["y"], me["x"]]
-        for d in (1, 3, 2):
-            total = total + r_three[h, d - 1]
+        for n in range(15):
+            total = total + r_two[h, n]
         half = slice(h * 128, h * 128 + 128)
         factor_v[:, half] = 4.0 * (first[:, half] - total)
 
     def rs_sent(group):
-        for name, counts in (("one", (3, 4, 4)), ("two", (1, 3, 4)), ("three", (1, 1, 3))):
-            sent((group[0][0], name), rs_whole(group, *counts))
+        sent((group[0][0], "one"), rs_whole(group, 3, 4, 4))
+        sent((group[0][0], "two"), r_two.at[group[0][2]])
 
     def partner_start(h):
         put("sum", ("sum", h), psend.at[h], precv.at[h], partner)
@@ -360,22 +351,21 @@
     adjoint_chunk(1 - k, 0, psend, True)
     partner_start(0)
     ag_ring_near(x_streams[1])
+    ag_ring_forward(z_streams)
     adjoint_chunk(k, 0, s_buf, False)
+    ag_ring_far(x_streams[1])
     partner_end(0)
     rs_one_start(s_streams[0])
-    ag_ring_far(x_streams[1])
-    ag_ring_forward(z_streams)
     ag_chip_wait(x_streams[1])
     split_factor(1)
     adjoint_chunk(1 - k, 1, psend, True)
     partner_start(1)
-    rs_one_forward(s_streams[0])
     ag_ring_near(z_streams)
     adjoint_chunk(k, 1, s_buf, False)
     partner_end(1)
     rs_one_start(s_streams[1])
+    rs_one_forward(s_streams[0])
     ag_ring_far(z_streams)
-    rs_one_end(s_streams[0])
 
     def split_weights(index, carry):
         core, y_lo, x = row_block(index)
@@ -426,13 +416,12 @@
 
     gram_tile(0, 0)
     gram_tile(0, 1)
-    rs_two_end(s_streams[0])
+    rs_one_end(s_streams[0])
     gram_tile(0, 2)
     gram_tile(0, 3)
     rs_one_end(s_streams[1])
     for q in range(4):
         gram_tile(1, q)
-    rs_two_end(s_streams[1])
 
     for i in range(8):
         ks[i] = weighted[2 * i : 2 * i + 2, :]
@@ -440,8 +429,8 @@
         y_to, z_to = at("y", y), at("z", d)
         put("k", "k", ks.at[(y_to // 2) * 4 + z_to], kb.at[c], device(me["x"], y_to, z_to, k))
     kb[c] = ks[c]
-    rs_three_end(s_streams[0])
-    rs_three_end(s_streams[1])
+    rs_two_end(s_streams[0])
+    rs_two_end(s_streams[1])
     factor_copy = pltpu.make_async_copy(factor_v, factor_out, local.at[0])
     factor_copy.start()
     got("k", kb.at[pl.ds(0, 7)])
@@ -460,10 +449,11 @@
     sent("k", ks.at[pl.ds(0, 7)])
     factor_copy.wait()
     core_copy.wait()
-    assert len(send_ids) <= SENDS and len(recv_ids) <= RECVS
-
-
-SENDS, RECVS = 22, 61
+    assert (len(send_ids), len(recv_ids)) == (SENDS, RECVS), (len(send_ids), len(recv_ids))
+
+
+PLANE = sorted(((i // 4, i % 4) for i in range(1, 16)), key=lambda p: -(2 - abs(2 - p[0]) + 2 - abs(2 - p[1])))
+SENDS, RECVS = 18, 44
 
 
 def write_out(core_ref, factor_ref, core_out, factor_out):
@@ -483,10 +473,10 @@
         scratch_shapes=[
             pltpu.VMEM((2, 512, 512), F32),
             pltpu.VMEM((2, 2, 8, 32, 1536), BF16),
-            pltpu.VMEM((4, 4, 512), F32),
+            pltpu.VMEM((4, 4, 2048), F32),
             pltpu.VMEM((4, 2, 512), F32),
             pltpu.VMEM((2, 2048), F32),
-            pltpu.VMEM((2, 2, 4, 4, 4, 16, 256), F32),
+            pltpu.VMEM((2, 2, 4, 4, 16, 1024), F32),
             pltpu.VMEM((2, 4, 4, 4, 8, 512), F32),
             pltpu.VMEM((2, 1024, 1024), BF16),
             pltpu.VMEM((2, 512, 1024), BF16),
@@ -494,8 +484,7 @@
             pltpu.VMEM((256, 768), BF16),
             pltpu.VMEM((8, 2, 256), F32),
             blocks, blocks, blocks, blocks, blocks, blocks, blocks,
-            pltpu.VMEM((2, 3, 4, 32, 128), F32),
-            pltpu.VMEM((2, 3, 32, 128), F32),
+            pltpu.VMEM((2, 15, 32, 128), F32),
             pltpu.VMEM((32, 256), F32),
             pltpu.VMEM((16, 256), F32),
             pltpu.VMEM((8, 2, 256), F32),

time: 60.1 us -> 55.4 us (0.922)
  Pallas kernels: 59.2 us -> 54.5 us
    pallas_call x1, Pallas kernels: 57.8 us -> 53.1 us  [on_device(): pl.pallas_call(kernel, out_shape=shapes, in_specs=[anywhere] * 3, out_spe...]
where the time goes in v4:
time: 55.4 us; the launch traced here: 55.2 us
  Pallas kernels  54.5 us (98%)
  between operations  0.64 us (1%)
    pallas_call x1, Pallas kernels, on_device(): pl.pallas_call(kernel, out_shape=shapes, in_specs=[anywhere] * 3, out_spe...  53.1 us
    pallas_call x1, Pallas kernels, on_device(): pl.pallas_call(write_out, out_shape=shapes, in_specs=[vmem, vmem], out_sp...  1.4 us

profile of v4, /device:TPU:0, one launch (start us, length us, event | category | flops | bytes accessed | tf_op | source)
XLA Modules:
  0.0 55.2 jit_solution(17305781004183480673)
XLA Ops:
  0.6 53.1 %shard_map.50 = (f32[2,2048]{1,0:T(2,128)}, f32[32,256]{1,0:T(8,128)}) custom-call(f32[4,2048]{1,0:T(4,128)} %x_hbm.1, f32[2,2048]{1,0:T(2,128)} %z_hbm.1, f32[2,512,512]{2,1,0:T(8,128)} %l_hbm.1), custom_call_target="tpu_custom_call" | custom-call | tf_op jit(solution)/shard_map/pallas_call | solution.py:468
  53.8 1.4 %shard_map.51 = (f32[2,2048]{1,0:T(2,128)}, f32[32,256]{1,0:T(8,128)}) custom-call(f32[2,2048]{1,0:T(2,128)} %get-tuple-element.4.core_ref, f32[32,256]{1,0:T(8,128)} %get-tuple-element.5.factor_ref), custom_call_target="tpu_custom_call" | custom-call | tf_op jit(solution)/shard_map/pallas_call | solution.py:502

commit v5 on v4

--- a/solution.py
+++ b/solution.py
@@ -16,7 +16,7 @@
 }
 ORDERS = ("xyz", "yzx", "zxy")
 S_PARTS = (
-    (pl.ds(0, 8), pl.ds(8, 8), pl.ds(16, 16)),
+    (pl.ds(0, 16), pl.ds(16, 8), pl.ds(24, 8)),
     (pl.ds(0, 8), pl.ds(8, 16), pl.ds(24, 8)),
 )
 
@@ -38,7 +38,7 @@
     x_hbm, z_hbm, l_hbm, core_out, factor_out,
     lbuf, lcat, xs, zs, zv, xb, zb, xcat, zcat, xct, zct, proj,
     psend, precv, s_buf, f_minus, f_plus, r_minus, r_plus, r_two,
-    first, weighted, ks, kb, core_v, factor_v, local, send, recv,
+    gram_v, first, weighted, ks, kb, core_v, factor_v, local, send, recv,
 ):
     r, c = lax.axis_index("row"), lax.axis_index("col")
     k = lax.rem(r, 2)
@@ -98,7 +98,7 @@
         copy.start()
     pl.semaphore_wait(barrier, len(greeted))
 
-    for d in (1, 3, 2):
+    for d in (2, 1, 3):
         put("xs", "xs", x_hbm, xs.at[me["z"]], peer("z", d))
     for d in (1, 3, 2):
         lanes = pl.ds(pl.multiple_of(at("z", d) * 512, 512), 512)
@@ -142,7 +142,7 @@
             name, order = stream[0], stream[5]
             axis, done = order[phase], {a: full for a in order[:phase]}
             here = block(stream, k, **done)
-            for d in (1, 3, 2):
+            for d in (2, 1, 3):
                 put((name, phase), (name, phase), here, here, peer(axis, d))
 
     def ag_direct_wait(group, phase):
@@ -220,37 +220,31 @@
     lax.fori_loop(0, 8, split_rows, 0)
     ag_direct_wait(x_streams[0], 0)
     ag_ring_start(x_streams[0])
+    lax.fori_loop(8, 16, split_rows, 0)
+    ag_direct_wait(x_streams[1], 0)
     ag_direct_wait(z_streams, 0)
+    ag_ring_forward(x_streams[0])
     ag_direct_start(z_streams, 1)
-    ag_direct_wait(x_streams[1], 0)
     ag_ring_start(x_streams[1])
-    lax.fori_loop(8, 16, split_rows, 0)
-    ag_ring_forward(x_streams[0])
     ag_ring_near(x_streams[0])
-    ag_direct_wait(z_streams, 1)
-    ag_ring_start(z_streams)
     ag_ring_far(x_streams[0])
     ag_ring_forward(x_streams[1])
-    ag_chip_wait(x_streams[0])
-
-    def row_block(index):
-        return lax.rem(index, 2), index // 8, lax.rem(index // 2, 4)
-
-    def split_factor(h):
+
+    def split_factor(h, core):
         def body(index, carry):
-            core, y_lo, x = row_block(index)
+            y_lo, x = index // 4, lax.rem(index, 4)
             for y_hi in range(2):
-                start = pl.multiple_of(index * 32 + y_hi * 16, 16)
+                start = pl.multiple_of((index * 2 + core) * 32 + y_hi * 16, 16)
                 for q in range(4):
                     hi, lo = split(xb[core, h, y_hi * 2 + y_lo, x, :, q * 256 : q * 256 + 256])
                     xcat[h, pl.ds(start, 16), q * 256 : q * 256 + 256] = hi
                     xcat[h, pl.ds(512 + start, 16), q * 256 : q * 256 + 256] = lo
             return carry
 
-        lax.fori_loop(0, 16, body, 0)
-
-    def adjoint_chunk(core, h, target, fresh):
-        for q in range(4):
+        lax.fori_loop(0, 8, body, 0)
+
+    def adjoint_chunk(core, h, target, fresh, tiles=(0, 1, 2, 3)):
+        for q in tiles:
             lanes = slice(q * 256, q * 256 + 256)
             rows = lcat[core].reshape(512, 1536)
             product = dot(rows[:, :1024], xcat[h, :, lanes]) + dot(rows[:, 1024:], xcat[h, 0:512, lanes])
@@ -347,28 +341,30 @@
         for z in range(4):
             s_buf[h, z] = s_buf[h, z] + precv[h, z]
 
-    split_factor(0)
+    split_factor(0, k)
+    ag_chip_wait(x_streams[0])
+    ag_direct_wait(z_streams, 1)
+    ag_ring_start(z_streams)
+    split_factor(0, 1 - k)
     adjoint_chunk(1 - k, 0, psend, True)
     partner_start(0)
     ag_ring_near(x_streams[1])
-    ag_ring_forward(z_streams)
     adjoint_chunk(k, 0, s_buf, False)
     ag_ring_far(x_streams[1])
+    split_factor(1, k)
     partner_end(0)
     rs_one_start(s_streams[0])
     ag_chip_wait(x_streams[1])
-    split_factor(1)
+    split_factor(1, 1 - k)
+    ag_ring_forward(z_streams)
     adjoint_chunk(1 - k, 1, psend, True)
     partner_start(1)
     ag_ring_near(z_streams)
+    rs_one_forward(s_streams[0])
     adjoint_chunk(k, 1, s_buf, False)
-    partner_end(1)
-    rs_one_start(s_streams[1])
-    rs_one_forward(s_streams[0])
-    ag_ring_far(z_streams)
 
     def split_weights(index, carry):
-        core, y_lo, x = row_block(index)
+        core, y_lo, x = lax.rem(index, 2), index // 8, lax.rem(index // 2, 4)
         start = pl.multiple_of(index * 16, 16)
         for h in range(2):
             for q in range(4):
@@ -392,36 +388,30 @@
             target[rows, 2 * depth : 3 * depth] = lo
 
     transpose(xcat, xct, 512)
+    partner_end(1)
+    rs_one_start(s_streams[1])
+
+    tiles = [(h, q, slice(q * 256, q * 256 + 256)) for h in range(2) for q in range(4)]
+    for h, q, lanes in tiles:
+        gram_v[h, q] = dot(xct[:, 0:1024], xcat[h, :, lanes]) + dot(xct[:, 1024:1536], xcat[h, 0:512, lanes])
+    ag_ring_far(z_streams)
+    rs_one_end(s_streams[0])
+    rs_one_forward(s_streams[1])
     ag_chip_wait(z_streams)
     lax.fori_loop(0, 16, split_weights, 0)
-    rs_one_forward(s_streams[1])
-    transpose(zcat, zct, 256)
-
-    first[...] = jnp.zeros_like(first)
-    weighted[...] = jnp.zeros_like(weighted)
     x_rows = [pl.ds(pl.multiple_of(base + r * 32, 32), 32) for base in (0, 512)]
     z_rows = [pl.ds(pl.multiple_of(base + r * 16, 16), 16) for base in (0, 256)]
 
-    def gram_tile(h, q):
-        lanes = slice(q * 256, q * 256 + 256)
-        gram = dot(xct[:, 0:1024], xcat[h, :, lanes]) + dot(xct[:, 1024:1536], xcat[h, 0:512, lanes])
-        core_gram = dot(zct[:, 0:512], zcat[h, :, lanes]) + dot(zct[:, 512:768], zcat[h, 0:256, lanes])
-        for total, source, rows, value in (
-            (first, xcat, x_rows, gram * core_gram),
-            (weighted, zcat, z_rows, gram * gram),
-        ):
-            hi, lo = split(value)
-            left_hi, left_lo = source[h, rows[0], lanes], source[h, rows[1], lanes]
-            total[...] += dot_nt(left_hi, hi) + dot_nt(left_hi, lo) + dot_nt(left_lo, hi)
-
-    gram_tile(0, 0)
-    gram_tile(0, 1)
-    rs_one_end(s_streams[0])
-    gram_tile(0, 2)
-    gram_tile(0, 3)
-    rs_one_end(s_streams[1])
-    for q in range(4):
-        gram_tile(1, q)
+    def times(source, rows, h, lanes, value):
+        hi, lo = split(value)
+        left_hi, left_lo = source[h, rows[0], lanes], source[h, rows[1], lanes]
+        return dot_nt(left_hi, hi) + dot_nt(left_hi, lo) + dot_nt(left_lo, hi)
+
+    total = jnp.zeros((16, 256), F32)
+    for h, q, lanes in tiles:
+        gram = gram_v[h, q]
+        total = total + times(zcat, z_rows, h, lanes, gram * gram)
+    weighted[...] = total
 
     for i in range(8):
         ks[i] = weighted[2 * i : 2 * i + 2, :]
@@ -429,15 +419,31 @@
         y_to, z_to = at("y", y), at("z", d)
         put("k", "k", ks.at[(y_to // 2) * 4 + z_to], kb.at[c], device(me["x"], y_to, z_to, k))
     kb[c] = ks[c]
-    rs_two_end(s_streams[0])
-    rs_two_end(s_streams[1])
-    factor_copy = pltpu.make_async_copy(factor_v, factor_out, local.at[0])
-    factor_copy.start()
+    transpose(zcat, zct, 256)
+
+    def core_tile(total, tile):
+        h, q, lanes = tile
+        core_gram = dot(zct[:, 0:512], zcat[h, :, lanes]) + dot(zct[:, 512:768], zcat[h, 0:256, lanes])
+        return total + times(xcat, x_rows, h, lanes, gram_v[h, q] * core_gram)
+
+    total = jnp.zeros((32, 256), F32)
+    for tile in tiles[:2]:
+        total = core_tile(total, tile)
+    first[...] = total
+    rs_one_end(s_streams[1])
+    total = first[...]
+    for tile in tiles[2:]:
+        total = core_tile(total, tile)
+    first[...] = total
     got("k", kb.at[pl.ds(0, 7)])
     for i in range(8):
         core_v[:, 256 * i : 256 * i + 256] = kb[i] - proj[i]
     core_copy = pltpu.make_async_copy(core_v, core_out, local.at[1])
     core_copy.start()
+    rs_two_end(s_streams[0])
+    rs_two_end(s_streams[1])
+    factor_copy = pltpu.make_async_copy(factor_v, factor_out, local.at[0])
+    factor_copy.start()
 
     sent("xs", xs.at[pl.ds(0, 3)])
     sent("zs", zs.at[pl.ds(0, 3)])
@@ -468,7 +474,7 @@
     results = pl.pallas_call(
         kernel,
         out_shape=shapes,
-        in_specs=[anywhere] * 3,
+        in_specs=[pl.BlockSpec(memory_space=pltpu.HBM)] * 3,
         out_specs=(anywhere, anywhere),
         scratch_shapes=[
             pltpu.VMEM((2, 512, 512), F32),
@@ -485,6 +491,7 @@
             pltpu.VMEM((8, 2, 256), F32),
             blocks, blocks, blocks, blocks, blocks, blocks, blocks,
             pltpu.VMEM((2, 15, 32, 128), F32),
+            pltpu.VMEM((2, 4, 256, 256), F32),
             pltpu.VMEM((32, 256), F32),
             pltpu.VMEM((16, 256), F32),
             pltpu.VMEM((8, 2, 256), F32),

time: 55.4 us -> 53.6 us (0.968)
  Pallas kernels: 54.5 us -> 52.8 us
    pallas_call x1, Pallas kernels: 53.1 us -> 51.4 us  [on_device(): pl.pallas_call(kernel, out_shape=shapes, in_specs=[pl.BlockSpec(memory_sp...]
where the time goes in v5:
time: 53.6 us; the launch traced here: 53.4 us
  Pallas kernels  52.8 us (99%)
  between operations  0.64 us (1%)
    pallas_call x1, Pallas kernels, on_device(): pl.pallas_call(kernel, out_shape=shapes, in_specs=[pl.BlockSpec(memory_sp...  51.4 us
    pallas_call x1, Pallas kernels, on_device(): pl.pallas_call(write_out, out_shape=shapes, in_specs=[vmem, vmem], out_sp...  1.4 us

profile of v5, /device:TPU:0, one launch (start us, length us, event | category | flops | bytes accessed | tf_op | source)
XLA Modules:
  0.0 53.4 jit_solution(11579413373207564436)
XLA Ops:
  0.6 51.4 %shard_map.50 = (f32[2,2048]{1,0:T(2,128)}, f32[32,256]{1,0:T(8,128)}) custom-call(f32[4,2048]{1,0:T(4,128)} %x_hbm.1, f32[2,2048]{1,0:T(2,128)} %z_hbm.1, f32[2,512,512]{2,1,0:T(8,128)} %l_hbm.1), custom_call_target="tpu_custom_call" | custom-call | tf_op jit(solution)/shard_map/pallas_call | solution.py:474
  52.0 1.4 %shard_map.51 = (f32[2,2048]{1,0:T(2,128)}, f32[32,256]{1,0:T(8,128)}) custom-call(f32[2,2048]{1,0:T(2,128)} %get-tuple-element.4.core_ref, f32[32,256]{1,0:T(8,128)} %get-tuple-element.5.factor_ref), custom_call_target="tpu_custom_call" | custom-call | tf_op jit(solution)/shard_map/pallas_call | solution.py:509

commit v6 on v5

--- a/solution.py
+++ b/solution.py
@@ -239,6 +239,7 @@
                     hi, lo = split(xb[core, h, y_hi * 2 + y_lo, x, :, q * 256 : q * 256 + 256])
                     xcat[h, pl.ds(start, 16), q * 256 : q * 256 + 256] = hi
                     xcat[h, pl.ds(512 + start, 16), q * 256 : q * 256 + 256] = lo
+                    xcat[h, pl.ds(1024 + start, 16), q * 256 : q * 256 + 256] = hi
             return carry
 
         lax.fori_loop(0, 8, body, 0)
@@ -247,7 +248,7 @@
         for q in tiles:
             lanes = slice(q * 256, q * 256 + 256)
             rows = lcat[core].reshape(512, 1536)
-            product = dot(rows[:, :1024], xcat[h, :, lanes]) + dot(rows[:, 1024:], xcat[h, 0:512, lanes])
+            product = dot(rows, xcat[h, :, lanes])
             starts = [(2 * q + e) * 256 + h * 128 for e in range(2)]
             weights = [
                 jnp.concatenate([zv[p : p + 1, at_ : at_ + 128] for at_ in starts], axis=1) for p in range(2)
@@ -393,7 +394,7 @@
 
     tiles = [(h, q, slice(q * 256, q * 256 + 256)) for h in range(2) for q in range(4)]
     for h, q, lanes in tiles:
-        gram_v[h, q] = dot(xct[:, 0:1024], xcat[h, :, lanes]) + dot(xct[:, 1024:1536], xcat[h, 0:512, lanes])
+        gram_v[h, q] = dot(xct[...], xcat[h, :, lanes])
     ag_ring_far(z_streams)
     rs_one_end(s_streams[0])
     rs_one_forward(s_streams[1])
@@ -484,7 +485,7 @@
             pltpu.VMEM((2, 2048), F32),
             pltpu.VMEM((2, 2, 4, 4, 16, 1024), F32),
             pltpu.VMEM((2, 4, 4, 4, 8, 512), F32),
-            pltpu.VMEM((2, 1024, 1024), BF16),
+            pltpu.VMEM((2, 1536, 1024), BF16),
             pltpu.VMEM((2, 512, 1024), BF16),
             pltpu.VMEM((256, 1536), BF16),
             pltpu.VMEM((256, 768), BF16),

time: 53.6 us -> 53.6 us (level)
  no operation moved by 1% of the time
where the time goes in v6:
time: 53.6 us; the launch traced here: 53.4 us
  Pallas kernels  52.8 us (99%)
  between operations  0.64 us (1%)
    pallas_call x1, Pallas kernels, on_device(): pl.pallas_call(kernel, out_shape=shapes, in_specs=[pl.BlockSpec(memory_sp...  51.4 us
    pallas_call x1, Pallas kernels, on_device(): pl.pallas_call(write_out, out_shape=shapes, in_specs=[vmem, vmem], out_sp...  1.4 us

profile of v6, /device:TPU:0, one launch (start us, length us, event | category | flops | bytes accessed | tf_op | source)
XLA Modules:
  0.0 53.4 jit_solution(4452809415606461857)
XLA Ops:
  0.6 51.4 %shard_map.50 = (f32[2,2048]{1,0:T(2,128)}, f32[32,256]{1,0:T(8,128)}) custom-call(f32[4,2048]{1,0:T(4,128)} %x_hbm.1, f32[2,2048]{1,0:T(2,128)} %z_hbm.1, f32[2,512,512]{2,1,0:T(8,128)} %l_hbm.1), custom_call_target="tpu_custom_call" | custom-call | tf_op jit(solution)/shard_map/pallas_call | solution.py:475
  52.0 1.4 %shard_map.51 = (f32[2,2048]{1,0:T(2,128)}, f32[32,256]{1,0:T(8,128)}) custom-call(f32[2,2048]{1,0:T(2,128)} %get-tuple-element.4.core_ref, f32[32,256]{1,0:T(8,128)} %get-tuple-element.5.factor_ref), custom_call_target="tpu_custom_call" | custom-call | tf_op jit(solution)/shard_map/pallas_call | solution.py:510
